TPU v7x, 512 devices: a whole 4x4x16 slice. The times are simulated.
512 devices in a mesh: cell: 64 (over x, z), col: 8 (over y, core).
Axes of the slice: x: 4, y: 4, z: 16, core: 2. Of those that a mesh axis runs over, the one named last changes fastest.
Arguments:
- panel_block: float32 [32768, 512], P('cell', 'col'), may hold values from -0.088388348 to 0.088388348, as said below
- trailing: float32 [32768, 7168], P('cell', 'col'), may hold values from -6 to 6
Outputs:
- triangle: float32 [512, 512], replicated
- coupling: float32 [512, 7168], P('cell', 'col')
- projected: float32 [32768, 7168], P('cell', 'col')
Inputs may be any that keep to these rules, and one draw needn't show every extreme that they name: `panel_block`: the panel has full column rank.
All inputs are finite; a program needn't handle non-finite values.
Results may differ from a plain program's by a relative error of at most 0.0003.
Values sent between devices are 32-bit elements; how exact they have to be, the bound alone decides.
No kernel may reach another device: no remote copies, remote signals or barrier semaphores. Data moves between devices by JAX's collectives and lax.ppermute only.
A program may use at most 64 MiB of HBM per device.

v0:
```python
import jax
import jax.numpy as jnp
from jax import lax
from jax.sharding import PartitionSpec as P


def contract_rows(left, right):
    return lax.dot_general(
        left,
        right,
        (((0,), (0,)), ((), ())),
        precision=lax.Precision.HIGHEST,
        preferred_element_type=jnp.float32,
    )


def on_device(panel_block, trailing):
    whole_panel = lax.all_gather(panel_block, "col", axis=1, tiled=True)
    gram = lax.psum(contract_rows(whole_panel, whole_panel), "cell")
    lower_factor = jnp.linalg.cholesky(gram)
    basis_t = jax.scipy.linalg.solve_triangular(
        lower_factor, jnp.transpose(whole_panel), lower=True
    )
    basis_rows = basis_t
    coupling = lax.psum_scatter(
        jnp.dot(
            basis_rows,
            trailing,
            precision=lax.Precision.HIGHEST,
            preferred_element_type=jnp.float32,
        ),
        "cell",
        scatter_dimension=0,
        tiled=True,
    )
    basis_rows = basis_t
    projected = trailing - contract_rows(
        basis_rows, lax.all_gather(coupling, "cell", axis=0, tiled=True)
    )
    triangle = jnp.transpose(lower_factor)
    return (triangle, coupling, projected)


def solution(mesh):
    placed = (P("cell", "col"), P("cell", "col"))
    return jax.shard_map(
        on_device,
        mesh=mesh,
        in_specs=placed,
        out_specs=(P(), P("cell", "col"), P("cell", "col")),
        check_vma=False,
    )
```

profile of v0, /device:TPU:24, one launch (start us, length us, event | category | flops | bytes accessed | tf_op | source)
XLA Modules:
  0.0 910.6 jit_solution(6047969047206828874)
XLA Ops:
  7.2 0.0 all-gather.3.cloned.1.call-start
  7.2 0.7 all-gather.3.cloned.1.call-update
  7.9 0.0 all-reduce.5.cloned.1.call-start
  7.9 36.0 %all-gather.3.cloned.1.call-done = f32[512,512]{0,1:T(8,128)} async-done(((f32[512,64]{0,1:T(8,128)}), f32[512,512]{0,1:T(8,128)}) %all-gather.3.cloned.1.call-update) | async-done | bytes 1048592 | tf_op jit(solution)/shard_map/all_gather | solution.py:18
  43.9 4.4 fusion.36
  48.3 0.0 all-reduce.5.cloned.1.call-update
  48.3 0.0 all-reduce.7.cloned.1.call-start
  48.4 277.5 %all-reduce.5.cloned.1.call-done = f32[512,512]{0,1:T(8,128)} async-done(((f32[512,512]{0,1:T(8,128)}), f32[512,512]{0,1:T(8,128)}) %all-reduce.5.cloned.1.call-update) | async-done | bytes 1048592 | tf_op jit(solution)/shard_map/psum | solution.py:19
  325.9 1.6 copy.9
  327.5 0.0 copy-done.2
  327.5 0.2 fusion
  327.8 11.7 %cholesky.104 = f32[128,128]{1,0:T(8,128)S(1)} custom-call(f32[128,128]{1,0:T(8,128)S(1)} %cholesky.266), custom_call_target="Cholesky" | custom-call | tf_op jit(solution)/shard_map/jit(cholesky)/cholesky | solution.py:20
  339.5 9.8 %custom-call.31 = f32[1,128,128]{1,2,0:T(8,128)S(1)} custom-call(f32[1,128,128]{2,1,0:T(8,128)S(1)} %get-tuple-element.38), custom_call_target="InvertDiagBlocksLowerTriangular" | custom-call | tf_op jit(solution)/shard_map/jit(cholesky)/cholesky | solution.py:20
  349.3 0.1 cholesky.224
  349.5 0.3 constant_dynamic-update-slice_fusion.3
  349.8 0.3 convolution_subtract_fusion.4
  350.1 11.7 %cholesky.217 = f32[128,128]{1,0:T(8,128)S(1)} custom-call(f32[128,128]{1,0:T(8,128)S(1)} %cholesky.270), custom_call_target="Cholesky" | custom-call | tf_op jit(solution)/shard_map/jit(cholesky)/cholesky | solution.py:20
  361.9 18.5 %custom-call.32 = f32[1,128,128]{1,2,0:T(8,128)S(1)} custom-call(f32[1,128,128]{2,1,0:T(8,128)S(1)} %get-tuple-element.35), custom_call_target="InvertDiagBlocksLowerTriangular" | custom-call | tf_op jit(solution)/shard_map/jit(cholesky)/cholesky | solution.py:20
  380.4 0.3 convolution_dynamic-update-slice_fusion
  380.6 0.4 convolution_subtract_fusion.5
  381.0 11.7 %cholesky.238 = f32[128,128]{1,0:T(8,128)S(1)} custom-call(f32[128,128]{1,0:T(8,128)S(1)} %cholesky.275), custom_call_target="Cholesky" | custom-call | tf_op jit(solution)/shard_map/jit(cholesky)/cholesky | solution.py:20
  392.8 0.7 compare_reduce_fusion.1
  393.5 9.8 %custom-call.33 = f32[1,128,128]{1,2,0:T(8,128)S(1)} custom-call(f32[1,128,128]{2,1,0:T(8,128)S(1)} %get-tuple-element.32), custom_call_target="InvertDiagBlocksLowerTriangular" | custom-call | tf_op jit(solution)/shard_map/jit(cholesky)/cholesky | solution.py:20
  403.3 0.2 convolution_dynamic-update-slice_fusion.1
  403.5 0.4 convolution_subtract_fusion.6
  403.9 11.7 %cholesky.255 = f32[128,128]{1,0:T(8,128)S(1)} custom-call(f32[128,128]{1,0:T(8,128)S(1)} %convolution_subtract_fusion.6), custom_call_target="Cholesky" | custom-call | tf_op jit(solution)/shard_map/jit(cholesky)/cholesky | solution.py:20
  415.7 0.6 compare_reduce_fusion
  416.3 0.6 compare_reduce_fusion.2
  419.5 0.0 copy-start
  419.5 1.4 fusion.1
  420.9 10.4 %while.1 = (s32[]{:T(128)}, f32[512,512]{1,0:T(8,128)S(1)}, s32[4,2]{0,1:T(2,128)S(1)}, f32[4,128,128]{2,1,0:T(8,128)}, s32[]{:T(128)}) while((s32[]{:T(128)}, f32[512,512]{1,0:T(8,128)S(1)}, s32[4,2]{0,1:T(2,128)S(1)}, f32[4,128,128]{2,1,0:T(8,128)}, s32[]{:T(128)}) %tuple.34), condition=%wide.while_cond, body=%wide.while_body.sunk | while | flops 2 | bytes 132205 | solution.py:21
  420.9 0.1 constant_dynamic-slice_fusion.3
  421.0 0.5 fusion.47
  421.5 2.0 bitcast_dynamic-update-slice_fusion.2
  423.5 0.1 constant_dynamic-slice_fusion.3
  423.6 0.5 fusion.47
  424.1 2.0 bitcast_dynamic-update-slice_fusion.2
  426.2 0.1 constant_dynamic-slice_fusion.3
  426.2 0.5 fusion.47
  426.7 2.0 bitcast_dynamic-update-slice_fusion.2
  428.8 0.1 constant_dynamic-slice_fusion.3
  428.8 0.5 fusion.47
  429.4 2.0 bitcast_dynamic-update-slice_fusion.2
  431.4 40.2 %custom-call.34 = f32[4,128,128]{1,2,0:T(8,128)S(1)} custom-call(f32[4,128,128]{2,1,0:T(8,128)} %get-tuple-element.10), custom_call_target="InvertDiagBlocksLowerTriangular" | custom-call | tf_op jit(solution)/shard_map/jit(_solve_triangular)/triangular_solve | solution.py:21
  471.6 0.0 copy-start.6
  471.6 0.0 copy-done
  471.6 0.4 fusion.12
  472.0 0.4 convolution_subtract_fusion.2
  472.4 0.4 fusion.25
  472.8 0.0 copy-start.1
  472.8 1.5 convolution_subtract_fusion.1
  474.3 1.3 fusion.23
  475.6 1.7 convolution_subtract_fusion.3
  477.2 1.3 fusion.22
  478.5 4.8 fusion.8
  483.3 0.0 all-reduce.7.cloned.1.call-update
  483.3 0.0 all-gather.5.cloned.1.call-start
  483.4 1.3 dynamic-slice.3
  485.3 273.0 %all-reduce.7.cloned.1.call-done = f32[512,896]{1,0:T(8,128)} async-done(((f32[512,896]{1,0:T(8,128)}), f32[512,896]{1,0:T(8,128)}) %all-reduce.7.cloned.1.call-update) | async-done | bytes 1835024
  758.3 1.4 constant_dynamic-slice_fusion.1
  759.6 0.0 all-gather.5.cloned.1.call-update
  759.7 2.5 copy.10
  762.2 135.3 %all-gather.5.cloned.1.call-done = f32[512,896]{1,0:T(8,128)} async-done(((f32[8,896]{1,0:T(8,128)}), f32[512,896]{1,0:T(8,128)}) %all-gather.5.cloned.1.call-update) | async-done | bytes 1835024 | tf_op jit(solution)/shard_map/all_gather | solution.py:38
  897.5 6.2 convolution_subtract_fusion
  (19 shorter events, 0.2 us)
Async XLA Ops:
  7.2 36.7 %all-gather.3.cloned.1.call-start = ((), (), s32[]{:S(2)}) async-start(), calls=%async_computation | async-start | bytes 1179648 | tf_op jit(solution)/shard_map/all_gather | solution.py:18
  7.9 318.0 %all-reduce.5.cloned.1.call-start = ((), (), s32[]{:S(2)}) async-start(), calls=%async_computation.1 | async-start | bytes 2097152 | tf_op jit(solution)/shard_map/psum | solution.py:19
  48.3 710.0 %all-reduce.7.cloned.1.call-start = ((), (), s32[]{:S(2)}) async-start(), calls=%async_computation.3 | async-start | bytes 3670016
  325.9 1.7 copy-start.2
  419.5 52.1 %copy-start = (f32[512,512]{0,1:T(8,128)S(1)}, f32[512,512]{0,1:T(8,128)}, u32[]{:S(2)}) copy-start(f32[512,512]{0,1:T(8,128)} %all-gather.3.cloned.1.call-done) | copy-start | bytes 3145732
  431.4 41.0 %copy-start.5 = (f32[512,512]{1,0:T(8,128)}, f32[512,512]{1,0:T(8,128)S(1)}, u32[]{:S(2)}) copy-start(f32[512,512]{1,0:T(8,128)S(1)} %get-tuple-element.97) | copy-start | bytes 3145732
  471.6 0.8 copy-start.6
  472.8 5.7 copy-start.1
  475.6 2.9 copy-start.3
  483.3 414.2 %copy-start.4 = (f32[128,512]{1,0:T(8,128)S(1)}, f32[128,512]{1,0:T(8,128)}, u32[]{:S(2)}) copy-start(f32[128,512]{1,0:T(8,128)} %copy-done.3) | copy-start | bytes 786436
  483.3 414.1 %all-gather.5.cloned.1.call-start = ((), (), s32[]{:S(2)}) async-start(), calls=%async_computation.2 | async-start | bytes 1863680 | tf_op jit(solution)/shard_map/all_gather | solution.py:38
Sparse Core Ops, SparseCore 0:
  10.1 33.7 all-gather.2
  48.4 277.3 all-reduce.4
  483.5 274.7 all-reduce.6
  761.7 135.7 all-gather.4
where the time goes:
time: 921 us; the launch traced here: 911 us
  waiting for transfers between devices  722 us (78%)
  other arithmetic  129 us (14%)
  matrix products  24.1 us (3%)
  between operations  17.6 us (2%)
  local copies, waits for them, and re-layouts  17.4 us (2%)
    psum x1, waiting for transfers between devices, on_device(): gram = lax.psum(contract_rows(whole_panel, whole_panel), 'cell')  277 us
    unnamed x5, waiting for transfers between devices  274 us
    all_gather x1, waiting for transfers between devices, on_device(): lax.all_gather(coupling, 'cell', axis=0, tiled=True)  135 us
    another operation x14, other arithmetic, on_device(): lower_factor = jnp.linalg.cholesky(gram)  87.1 us
    another operation x3, other arithmetic, on_device(): jax.scipy.linalg.solve_triangular(lower_factor, jnp.transpose(whole_panel...  41.6 us
    all_gather x1, waiting for transfers between devices, on_device(): whole_panel = lax.all_gather(panel_block, 'col', axis=1, tiled=True)  36 us
  transfers between devices with their start and end apart: 4, of which 4 were waited for; matrix products, arithmetic and copies ran while one was open for 0% of the time, Pallas kernels for 0%

commit v1 on v0

v1 whole, which is shorter than its diff:
```python
import functools
import jax, jax.numpy as jnp
from jax import lax
from jax.sharding import Mesh
from jax.sharding import PartitionSpec as P
from jax.experimental import pallas as pl
from jax.experimental.pallas import tpu as pltpu

HI = lax.Precision.HIGHEST
NB = 128

def mxu(a, b, dims):
    return lax.dot_general(a, b, (dims, ((), ())), precision=HI, preferred_element_type=jnp.float32)

def factor_block(s_full, rows_ref):
    G = NB // 8
    sub = lax.broadcasted_iota(jnp.int32, (8, NB), 0)
    lane = lax.broadcasted_iota(jnp.int32, (8, NB), 1)
    s = [s_full[8 * g : 8 * g + 8, :] for g in range(G)]
    v = [jnp.where(lane == sub + 8 * g, 1.0, 0.0).astype(jnp.float32) for g in range(G)]
    for k in range(NB):
        g0, i0 = k // 8, k % 8
        col = [jnp.broadcast_to(s[g][:, k : k + 1], (8, NB)) for g in range(g0, G)]
        r = s[g0][i0 : i0 + 1, :]
        rows_ref[k : k + 1, :] = r
        if k == NB - 1:
            break
        inv = 1.0 / col[0][i0 : i0 + 1, :]
        rd = jnp.broadcast_to(r * inv, (8, NB))
        vd = jnp.broadcast_to(v[g0][i0 : i0 + 1, :] * inv, (8, NB))
        for g in range(g0, G):
            c = col[g - g0]
            if g == g0:
                if i0 == 7:
                    continue
                c = jnp.where(sub > i0, c, 0.0)
            s[g] = s[g] - c * rd
            v[g] = v[g] - c * vd
    return jnp.concatenate(v, axis=0)

def kernel(n, g_ref, r_ref, x_ref, a, rows):
    w = 2 * n
    a[:, :n] = g_ref[...]
    a[:, n:] = jnp.where(lax.broadcasted_iota(jnp.int32, (n, n), 0) == lax.broadcasted_iota(jnp.int32, (n, n), 1), 1.0, 0.0)
    sub = lax.broadcasted_iota(jnp.int32, (NB, NB), 0)
    lane = lax.broadcasted_iota(jnp.int32, (NB, NB), 1)
    wide = lax.broadcasted_iota(jnp.int32, (NB, n), 1)
    high = lax.broadcasted_iota(jnp.int32, (NB, n), 0)

    def step(kb, carry):
        at = pl.multiple_of(kb * NB, NB)
        v = factor_block(a[pl.ds(at, NB), pl.ds(at, NB)], rows)
        rt = rows[...]
        d = jnp.sum(jnp.where(sub == lane, rt, 0.0), axis=1, keepdims=True)
        linv = v * lax.rsqrt(d)
        out = mxu(linv, a[pl.ds(at, NB), :], ((1,), (0,)))
        x_ref[pl.ds(at, NB), :] = out[:, n:]
        r_ref[pl.ds(at, NB), :] = jnp.where(wide >= at + high, out[:, :n], 0.0)
        rm = jnp.where(wide >= at + NB, out[:, :n], 0.0)
        out = jnp.concatenate([rm, out[:, n:]], axis=1)
        a[...] -= mxu(rm, out, ((0,), (0,)))
        return carry

    lax.fori_loop(0, n // NB, step, 0)

def chol_inv(g):
    n = g.shape[0]
    return pl.pallas_call(
        functools.partial(kernel, n),
        out_shape=(jax.ShapeDtypeStruct((n, n), jnp.float32),) * 2,
        in_specs=[pl.BlockSpec(memory_space=pltpu.VMEM)],
        out_specs=[pl.BlockSpec(memory_space=pltpu.VMEM)] * 2,
        scratch_shapes=[pltpu.VMEM((n, 2 * n), jnp.float32), pltpu.VMEM((NB, NB), jnp.float32)],
        compiler_params=pltpu.CompilerParams(vmem_limit_bytes=32 << 20),
    )(g)


def join_cores(part):
    half = part.shape[0] // 2
    both = []
    for block in (part[:half], part[half:]):
        pair = lax.all_gather(block, "core", axis=0, tiled=False)
        both.append(jnp.swapaxes(pair.reshape(2, 2, 64, -1), 0, 1))
    return jnp.concatenate(both, axis=0).reshape(2 * part.shape[0], -1)


def on_device(panel_block, trailing):
    width = trailing.shape[1]
    panel_t = join_cores(
        lax.all_gather(jnp.transpose(panel_block), "y", axis=0, tiled=True)
    )
    partial = jnp.concatenate(
        [
            mxu(panel_t, trailing, ((1,), (0,))),
            mxu(panel_t, panel_block, ((1,), (0,))),
        ],
        axis=1,
    )
    full = partial.shape[1]
    over_x = lax.all_to_all(
        partial.reshape(4, 128, full), "x", 0, 0, tiled=True
    )
    over_x = jnp.sum(over_x, axis=0).reshape(4, 4, 8, full)
    over_l = lax.all_to_all(
        jnp.swapaxes(over_x, 0, 1), "zl", 0, 0, tiled=True
    )
    over_l = jnp.sum(over_l, axis=0)
    over_h = lax.all_to_all(over_l, "zh", 0, 0, tiled=True)
    own = jnp.sum(over_h, axis=0)
    back_h = lax.all_gather(own, "zh", axis=0, tiled=False)
    back_l = lax.all_gather(back_h, "zl", axis=1, tiled=False)
    back_z = back_l.reshape(1, 128, full)
    whole = lax.all_to_all(
        jnp.broadcast_to(back_z, (4, 128, full)), "x", 0, 0, tiled=True
    ).reshape(512, full)
    gram = join_cores(
        lax.all_gather(
            jnp.transpose(whole[:, width:]), "y", axis=0, tiled=True
        )
    )
    triangle, inverse = chol_inv(gram)
    basis_t = mxu(inverse, panel_t, ((1,), (0,)))
    coupling = mxu(inverse, whole[:, :width], ((1,), (0,)))
    projected = trailing - mxu(basis_t, coupling, ((0,), (0,)))
    row = 128 * lax.axis_index("x") + 32 * lax.axis_index("zh")
    row = row + 8 * lax.axis_index("zl")
    return (
        triangle,
        lax.dynamic_slice_in_dim(coupling, row, 8, axis=0),
        projected,
    )


def solution(mesh):
    fine = Mesh(
        mesh.devices.reshape(4, 4, 4, 4, 2), ("x", "zh", "zl", "y", "core")
    )
    cell, col = ("x", "zh", "zl"), ("y", "core")
    placed = P(cell, col)
    return jax.shard_map(
        on_device,
        mesh=fine,
        in_specs=(placed, placed),
        out_specs=(P(), placed, placed),
        check_vma=False,
    )
```

time: 921 us -> 240 us (0.26); the launches traced: 911 us -> 239 us
  waiting for transfers between devices: 722 us -> 17.2 us
  blocking collectives: 0 us -> 144 us
  other arithmetic: 129 us -> 0.63 us
  Pallas kernels: 0 us -> 52.2 us
  between operations: 17.6 us -> 0.82 us
  local copies, waits for them, and re-layouts: 17.4 us -> 5.48 us
  matrix products: 24.1 us -> 14.7 us
    psum x1 -> x0, waiting for transfers between devices: 277 us -> none  [on_device(): gram = lax.psum(contract_rows(whole_panel, whole_panel), 'cell')]
    unnamed x5 -> x0, waiting for transfers between devices: 274 us -> none
    all_gather x2 -> x0, waiting for transfers between devices: 171 us -> none  [the longest x1 135 us: on_device(): lax.all_gather(coupling, 'cell', axis=0, tiled=True)]
    another operation x17 -> x0, other arithmetic: 129 us -> none  [the longest x14 87.1 us: on_device(): lower_factor = jnp.linalg.cholesky(gram)]
    all_to_all x0 -> x3, blocking collectives: none -> 72.8 us  [the longest x1 29.1 us: on_device(): lax.all_to_all(partial.reshape(4, 128, full), 'x', 0, 0, tiled=True)]
    all_gather x0 -> x8, blocking collectives: none -> 71.4 us  [the longest x1 18.3 us: on_device(): back_h = lax.all_gather(own, 'zh', axis=0, tiled=False)]
    pallas_call x0 -> x1, Pallas kernels: none -> 52.2 us  [chol_inv(): pl.pallas_call(functools.partial(kernel, n), out_shape=(jax.ShapeDtypeStr...]
    all_to_all x0 -> x1, waiting for transfers between devices: none -> 17.2 us  [on_device(): lax.all_to_all(jnp.broadcast_to(back_z, (4, 128, full)), 'x', 0, 0, tiled...]
  transfers between devices with their start and end apart: 4 -> 1, of which waited for: 4 -> 1; matrix products, arithmetic and copies ran while one was open for 0% -> 0% of each run, Pallas kernels for 0% -> 0%
where the time goes in v1:
time: 240 us; the launch traced here: 239 us
  blocking collectives  144 us (60%)
  Pallas kernels  52.2 us (22%)
  waiting for transfers between devices  17.2 us (7%)
  matrix products  14.7 us (6%)
  local copies, waits for them, and re-layouts  5.48 us (2%)
  starting transfers between devices  3.6 us (2%)
    pallas_call x1, Pallas kernels, chol_inv(): pl.pallas_call(functools.partial(kernel, n), out_shape=(jax.ShapeDtypeStr...  52.2 us
    all_to_all x1, blocking collectives, on_device(): lax.all_to_all(partial.reshape(4, 128, full), 'x', 0, 0, tiled=True)  29.1 us
    all_to_all x1, blocking collectives, on_device(): over_h = lax.all_to_all(over_l, 'zh', 0, 0, tiled=True)  26 us
    all_gather x1, blocking collectives, on_device(): back_h = lax.all_gather(own, 'zh', axis=0, tiled=False)  18.3 us
    all_to_all x1, blocking collectives, on_device(): over_l = lax.all_to_all(jnp.swapaxes(over_x, 0, 1), 'zl', 0, 0, tiled=True)  17.8 us
    all_to_all x1, waiting for transfers between devices, on_device(): lax.all_to_all(jnp.broadcast_to(back_z, (4, 128, full)), 'x', 0, 0, tiled...  17.2 us
    all_gather x1, blocking collectives, on_device(): back_l = lax.all_gather(back_h, 'zl', axis=1, tiled=False)  16.1 us
    all_gather x1, blocking collectives, on_device(): lax.all_gather(jnp.transpose(panel_block), 'y', axis=0, tiled=True)  15.4 us
  transfers between devices with their start and end apart: 1, of which 1 were waited for; matrix products, arithmetic and copies ran while one was open for 0% of the time, Pallas kernels for 0%

profile of v1, /device:TPU:24, one launch (start us, length us, event | category | flops | bytes accessed | tf_op | source)
XLA Modules:
  0.0 238.8 jit_solution(12380002667436966053)
XLA Ops:
  0.6 15.4 %all_gather.42 = f32[256,512]{1,0:T(8,128)S(1)} all-gather(f32[64,512]{1,0:T(8,128)} %bitcast.49), channel_id=1, replica_groups=mesh['x'=4,'zh'=4,'zl'=4,'y'=4,'core'=2] {'y'}, dimensions={0}, use_global_device_ids=true | all-gather | bytes 655360 | tf_op jit(solution)/shard_map/all_gather | solution.py:90
  16.1 2.2 all-gather.1
  18.3 2.2 all-gather
  20.4 0.0 copy-start.2
  20.4 0.1 pad_maximum_fusion.1
  20.5 0.0 copy-start
  20.6 0.1 copy.33
  20.7 0.7 copy-done.2
  21.3 1.0 fusion.5
  22.3 0.0 copy-done
  22.3 3.6 %fusion.4 = f32[512,896]{1,0:T(8,128)S(1)} fusion(f32[512,512]{1,0:T(8,128)S(1)} %bitcast.39, f32[512,896]{1,0:T(8,128)S(1)} %copy-done), kind=kOutput, calls=%fused_computation.11 | convolution fusion | flops 2818572288 | bytes 4718592 | tf_op jit(solution)/shard_map/dot_general | solution.py:13
  25.9 0.2 pad_maximum_fusion
  26.1 1.8 copy.35
  28.0 29.1 %all_to_all.20 = f32[4,128,960]{1,2,0:T(8,128)S(1)} all-to-all(f32[4,128,960]{1,2,0:T(8,128)} %copy.35), channel_id=1, replica_groups=mesh['x'=4,'zh'=4,'zl'=4,'y'=4,'core'=2] {'x'}, dimensions={0} | all-to-all | bytes 3932160 | tf_op jit(solution)/shard_map/all_to_all | solution.py:100
  57.0 0.1 reduce_sum.27
  57.2 0.2 copy.36
  57.4 17.8 %all_to_all.21 = f32[4,4,8,960]{3,2,1,0:T(8,128)S(1)} all-to-all(f32[4,4,8,960]{3,2,1,0:T(8,128)S(1)} %copy.37), channel_id=1, replica_groups=mesh['x'=4,'zh'=4,'zl'=4,'y'=4,'core'=2] {'zl'}, dimensions={0} | all-to-all | bytes 983040 | tf_op jit(solution)/shard_map/all_to_all | solution.py:104
  75.2 26.0 %all_to_all.22 = f32[4,8,960]{2,1,0:T(8,128)S(1)} all-to-all(f32[4,8,960]{2,1,0:T(8,128)S(1)} %reduce_sum.28), channel_id=1, replica_groups=mesh['x'=4,'zh'=4,'zl'=4,'y'=4,'core'=2] {'zh'}, dimensions={0} | all-to-all | bytes 245760 | tf_op jit(solution)/shard_map/all_to_all | solution.py:108
  101.2 18.3 %all-gather.2 = f32[32,960]{1,0:T(8,128)S(1)} all-gather(f32[8,960]{1,0:T(8,128)S(1)} %reduce_sum.29), channel_id=4, replica_groups=mesh['x'=4,'zh'=4,'zl'=4,'y'=4,'core'=2] {'zh'}, dimensions={0}, use_global_device_ids=true | all-gather | bytes 153600 | tf_op jit(solution)/shard_map/all_gather | solution.py:110
  119.5 16.1 %all-gather.3 = f32[4,32,960]{2,1,0:T(8,128)S(1)} all-gather(f32[4,8,960]{2,1,0:T(8,128)S(1)} %bitcast.48), channel_id=5, replica_groups=mesh['x'=4,'zh'=4,'zl'=4,'y'=4,'core'=2] {'zl'}, dimensions={1}, use_global_device_ids=true | all-gather | bytes 614400 | tf_op jit(solution)/shard_map/all_gather | solution.py:111
  135.6 0.2 copy.38
  135.8 1.4 broadcast_in_dim.8
  137.2 3.6 %all-to-all-start.3 = ((f32[4,128,960]{1,2,0:T(8,128)}), f32[4,128,960]{1,2,0:T(8,128)S(1)}, u32[]{:S(2)}, u32[]{:S(2)}) async-start(f32[4,128,960]{1,2,0:T(8,128)} %broadcast_in_dim.8), calls=%async_computation.3 | async-start | bytes 3932160 | tf_op jit(solution)/shard_map/all_to_all | solution.py:113
  140.8 17.2 %all-to-all-done.3 = f32[4,128,960]{1,2,0:T(8,128)S(1)} async-done(((f32[4,128,960]{1,2,0:T(8,128)}), f32[4,128,960]{1,2,0:T(8,128)S(1)}, u32[]{:S(2)}, u32[]{:S(2)}) %all-to-all-start.3) | async-done | bytes 1966112 | tf_op jit(solution)/shard_map/all_to_all | solution.py:113
  158.0 0.3 copy_bitcast_fusion
  158.3 12.8 %all_gather.51 = f32[256,512]{1,0:T(8,128)S(1)} all-gather(f32[64,512]{1,0:T(8,128)S(1)} %slice_bitcast_fusion), channel_id=1, replica_groups=mesh['x'=4,'zh'=4,'zl'=4,'y'=4,'core'=2] {'y'}, dimensions={0}, use_global_device_ids=true | all-gather | bytes 655360 | tf_op jit(solution)/shard_map/all_gather | solution.py:117
  171.1 2.2 all-gather.5
  173.3 2.3 all-gather.4
  175.6 0.1 pad_maximum_fusion.2
  175.7 0.1 copy.40
  175.8 52.2 %shard_map.49 = (f32[512,512]{1,0:T(8,128)}, f32[512,512]{1,0:T(8,128)S(1)}) custom-call(f32[512,512]{1,0:T(8,128)S(1)} %bitcast.37), custom_call_target="tpu_custom_call" | custom-call | tf_op jit(solution)/shard_map/pallas_call | solution.py:68
  228.0 3.5 %fusion = f32[512,896]{1,0:T(8,128)S(1)} fusion(f32[512,512]{1,0:T(8,128)S(1)} %get-tuple-element.6, f32[512,960]{0,1:T(8,128)S(1)} %copy_bitcast_fusion), kind=kOutput, calls=%fused_computation.2 | convolution fusion | flops 2818572288 | bytes 4718592 | tf_op jit(solution)/shard_map/dot_general | solution.py:13
  231.5 0.0 copy-start.1
  231.6 1.8 fusion.6
  233.4 0.6 constant_dynamic-slice_fusion
  234.0 0.0 copy-done.1
  234.0 4.8 %convolution_subtract_fusion = f32[512,896]{1,0:T(8,128)} fusion(f32[512,896]{1,0:T(8,128)S(1)} %copy-done.1, f32[512,512]{1,0:T(8,128)S(1)} %fusion.6, f32[512,896]{1,0:T(8,128)S(1)} %fusion), kind=kOutput, calls=%fused_computation.4 | convolution fusion | flops 2819031040 | bytes 6553600 | tf_op jit(solution)/shard_map/dot_general | solution.py:13
  (6 shorter events, 0.2 us)
Async XLA Ops:
  20.4 0.9 copy-start.2
  20.5 1.8 copy-start
  137.2 20.8 %all-to-all-start.3 = ((f32[4,128,960]{1,2,0:T(8,128)}), f32[4,128,960]{1,2,0:T(8,128)S(1)}, u32[]{:S(2)}, u32[]{:S(2)}) async-start(f32[4,128,960]{1,2,0:T(8,128)} %broadcast_in_dim.8), calls=%async_computation.3 | async-start | bytes 3932160 | tf_op jit(solution)/shard_map/all_to_all | solution.py:113
  231.5 2.5 %copy-start.1 = (f32[512,896]{1,0:T(8,128)S(1)}, f32[512,896]{1,0:T(8,128)}, u32[]{:S(2)}) copy-start(f32[512,896]{1,0:T(8,128)} %param.3) | copy-start | bytes 5505028

commit v2 on v1

v2 whole, which is shorter than its diff:
```python
import functools
import jax, jax.numpy as jnp
from jax import lax
from jax.sharding import Mesh
from jax.sharding import PartitionSpec as P
from jax.experimental import pallas as pl
from jax.experimental.pallas import tpu as pltpu

HI = lax.Precision.HIGHEST
NB = 128


def mxu(a, b, dims):
    return lax.dot_general(a, b, (dims, ((), ())), precision=HI, preferred_element_type=jnp.float32)


def factor_block(s_full, rows_ref):
    G = NB // 8
    sub = lax.broadcasted_iota(jnp.int32, (8, NB), 0)
    lane = lax.broadcasted_iota(jnp.int32, (8, NB), 1)
    s = [s_full[8 * g : 8 * g + 8, :] for g in range(G)]
    v = [jnp.where(lane == sub + 8 * g, 1.0, 0.0).astype(jnp.float32) for g in range(G)]
    for k in range(NB):
        g0, i0 = k // 8, k % 8
        col = [jnp.broadcast_to(s[g][:, k : k + 1], (8, NB)) for g in range(g0, G)]
        r = s[g0][i0 : i0 + 1, :]
        rows_ref[k : k + 1, :] = r
        if k == NB - 1:
            break
        inv = 1.0 / col[0][i0 : i0 + 1, :]
        rd = jnp.broadcast_to(r * inv, (8, NB))
        vd = jnp.broadcast_to(v[g0][i0 : i0 + 1, :] * inv, (8, NB))
        for g in range(g0, G):
            c = col[g - g0]
            if g == g0:
                if i0 == 7:
                    continue
                c = jnp.where(sub > i0, c, 0.0)
            s[g] = s[g] - c * rd
            v[g] = v[g] - c * vd
    return jnp.concatenate(v, axis=0)


def start_kernel(n, g_ref, a_ref):
    a_ref[:, :n] = g_ref[...]
    row = lax.broadcasted_iota(jnp.int32, (n, n), 0)
    a_ref[:, n:] = jnp.where(row == lax.broadcasted_iota(jnp.int32, (n, n), 1), 1.0, 0.0)


def steps_kernel(n, first, last, *refs):
    if first == 0:
        g_ref, a, rows = refs
        start_kernel(n, g_ref, a)
    else:
        _, a, rows = refs
    sub = lax.broadcasted_iota(jnp.int32, (NB, NB), 0)
    lane = lax.broadcasted_iota(jnp.int32, (NB, NB), 1)
    wide = lax.broadcasted_iota(jnp.int32, (NB, n), 1)
    high = lax.broadcasted_iota(jnp.int32, (NB, n), 0)
    tall = lax.broadcasted_iota(jnp.int32, (n, n), 0)

    def step(kb, carry):
        at = pl.multiple_of(kb * NB, NB)
        v = factor_block(a[pl.ds(at, NB), pl.ds(at, NB)], rows)
        rt = rows[...]
        d = jnp.sum(jnp.where(sub == lane, rt, 0.0), axis=1, keepdims=True)
        linv = v * lax.rsqrt(d)
        out = mxu(linv, a[pl.ds(at, NB), :], ((1,), (0,)))
        rm = jnp.where(wide >= at + NB, out[:, :n], 0.0)
        full = jnp.concatenate([rm, out[:, n:]], axis=1)
        a[...] -= mxu(rm, full, ((0,), (0,)))
        a[pl.ds(at, NB), n:] = out[:, n:]
        a[pl.ds(at, NB), :n] = jnp.where(wide >= at + high, out[:, :n], 0.0)
        return carry

    lax.fori_loop(first, last, step, 0)


def factor_steps(n, first, last, x):
    cost = pl.CostEstimate(
        flops=(last - first) * 2 * 6 * n * n * n // 2, bytes_accessed=4 * n * n * 4, transcendentals=0
    )
    return pl.pallas_call(
        functools.partial(steps_kernel, n, first, last),
        out_shape=jax.ShapeDtypeStruct((n, 2 * n), jnp.float32),
        in_specs=[pl.BlockSpec(memory_space=pltpu.VMEM)],
        out_specs=pl.BlockSpec(memory_space=pltpu.VMEM),
        scratch_shapes=[pltpu.VMEM((NB, NB), jnp.float32)],
        input_output_aliases={} if first == 0 else {0: 0},
        cost_estimate=cost,
        compiler_params=pltpu.CompilerParams(vmem_limit_bytes=32 << 20),
    )(x)


def join_cores(part):
    half = part.shape[0] // 2
    both = []
    for block in (part[:half], part[half:]):
        pair = lax.all_gather(block, "core", axis=0, tiled=False)
        both.append(jnp.swapaxes(pair.reshape(2, 2, 64, -1), 0, 1))
    return jnp.concatenate(both, axis=0).reshape(2 * part.shape[0], -1)


CELL = ("x", "z")


def exchange(blocks, axes):
    return lax.all_to_all(blocks, axes, 0, 0, tiled=True)


def on_device(panel_block, trailing):
    width = trailing.shape[1]
    block_t = jnp.transpose(panel_block)
    panel_t = join_cores(lax.all_gather(block_t, "y", axis=0, tiled=True))
    partial = mxu(panel_t, trailing, ((1,), (0,)))
    gram = mxu(block_t, panel_t, ((1,), (1,)))
    blocks, here = partial.reshape(4, 128, width), lax.axis_index("x")
    away = [
        lax.ppermute(
            lax.dynamic_index_in_dim(blocks, (here + k) % 4, 0, False),
            "x",
            [(i, (i + k) % 4) for i in range(4)],
        )
        for k in (1, 2, 3)
    ]
    c = lax.dynamic_index_in_dim(blocks, here, 0, False)
    c = (c + away[1]) + (away[0] + away[2])
    c = exchange(c.reshape(16, 8, width), "z")
    c = jnp.sum(c, axis=0)
    c = exchange(jnp.broadcast_to(c[None], (16, 8, width)), "z")
    c = exchange(jnp.broadcast_to(c.reshape(1, 128, width), (4, 128, width)), "x")
    c = c.reshape(512, width)
    gram = exchange(gram.reshape(64, 1, 512), CELL)
    gram = jnp.sum(gram, axis=0)
    gram = lax.all_gather(gram, "z", axis=0, tiled=False)
    gram = lax.all_gather(gram, "x", axis=0, tiled=False)
    gram = join_cores(lax.all_gather(gram.reshape(64, 512), "y", axis=0, tiled=True))
    state = factor_steps(512, 0, 2, gram)
    state = factor_steps(512, 2, 4, state)
    triangle, inverse = state[:, :512], state[:, 512:]
    basis_t = mxu(inverse, panel_t, ((1,), (0,)))
    coupling = mxu(inverse, c, ((1,), (0,)))
    projected = trailing - mxu(basis_t, coupling, ((0,), (0,)))
    row = 128 * lax.axis_index("x") + 8 * lax.axis_index("z")
    mine = lax.dynamic_slice_in_dim(coupling, row, 8, axis=0)
    return (triangle, mine, projected)


def solution(mesh):
    fine = Mesh(mesh.devices.reshape(4, 16, 4, 2), ("x", "z", "y", "core"))
    placed = P(CELL, ("y", "core"))
    return jax.shard_map(
        on_device,
        mesh=fine,
        in_specs=(placed, placed),
        out_specs=(P(), placed, placed),
        check_vma=False,
    )
```

time: 240 us -> 274 us (1.14)
  blocking collectives: 144 us -> 93.5 us
  waiting for transfers between devices: 17.2 us -> 57.2 us
  starting transfers between devices: 3.6 us -> 41.3 us
  matrix products: 14.7 us -> 19 us
    all_to_all x3 -> x0, blocking collectives: 72.8 us -> none  [the longest x1 29.1 us: on_device(): lax.all_to_all(partial.reshape(4, 128, full), 'x', 0, 0, tiled=True)]
    all_to_all x1 -> x4, starting transfers between devices: 3.6 us -> 30.9 us  [exchange(): return lax.all_to_all(blocks, axes, 0, 0, tiled=True)]
    all_to_all x1 -> x4, waiting for transfers between devices: 17.2 us -> 41.3 us  [exchange(): return lax.all_to_all(blocks, axes, 0, 0, tiled=True)]
    all_gather x4, blocking collectives: 62.5 us -> 84.6 us  [the longest x1 44.4 us: on_device(): gram = lax.all_gather(gram, 'z', axis=0, tiled=False)]
    ppermute x0 -> x3, waiting for transfers between devices: none -> 15.9 us  [on_device(): lax.ppermute(lax.dynamic_index_in_dim(blocks, (here + k) % 4, 0, False),...]
    ppermute x0 -> x3, starting transfers between devices: none -> 10.3 us  [on_device(): lax.ppermute(lax.dynamic_index_in_dim(blocks, (here + k) % 4, 0, False),...]
    dot_general x5, matrix products: 14.7 us -> 19 us  [mxu(): lax.dot_general(a, b, (dims, ((), ())), precision=HI, preferred_element_t...]
    pallas_call x1 -> x2, Pallas kernels: 52.2 us -> 52.3 us  [factor_steps(): pl.pallas_call(functools.partial(steps_kernel, n, first, last), out_shape...]
  transfers between devices with their start and end apart: 1 -> 7, of which waited for: 1 -> 4; matrix products, arithmetic and copies ran while one was open for 0% -> 2% of each run, Pallas kernels for 0% -> 19%
where the time goes in v2:
time: 274 us; the launch traced here: 272 us
  blocking collectives  93.5 us (34%)
  waiting for transfers between devices  57.2 us (21%)
  Pallas kernels  52.3 us (19%)
  starting transfers between devices  41.3 us (15%)
  matrix products  19 us (7%)
  local copies, waits for them, and re-layouts  5.99 us (2%)
    pallas_call x2, Pallas kernels, factor_steps(): pl.pallas_call(functools.partial(steps_kernel, n, first, last), out_shape...  52.3 us
    all_gather x1, blocking collectives, on_device(): gram = lax.all_gather(gram, 'z', axis=0, tiled=False)  44.4 us
    all_to_all x4, waiting for transfers between devices, exchange(): return lax.all_to_all(blocks, axes, 0, 0, tiled=True)  41.3 us
    all_to_all x4, starting transfers between devices, exchange(): return lax.all_to_all(blocks, axes, 0, 0, tiled=True)  30.9 us
    dot_general x5, matrix products, mxu(): lax.dot_general(a, b, (dims, ((), ())), precision=HI, preferred_element_t...  19 us
    ppermute x3, waiting for transfers between devices, on_device(): lax.ppermute(lax.dynamic_index_in_dim(blocks, (here + k) % 4, 0, False),...  15.9 us
    all_gather x1, blocking collectives, on_device(): panel_t = join_cores(lax.all_gather(block_t, 'y', axis=0, tiled=True))  15.4 us
    all_gather x1, blocking collectives, on_device(): lax.all_gather(gram.reshape(64, 512), 'y', axis=0, tiled=True)  12.8 us
  transfers between devices with their start and end apart: 7, of which 4 were waited for; matrix products, arithmetic and copies ran while one was open for 2% of the time, Pallas kernels for 19%

profile of v2, /device:TPU:24, one launch (start us, length us, event | category | flops | bytes accessed | tf_op | source)
XLA Modules:
  0.0 272.3 jit_solution(17176588322635841673)
XLA Ops:
  0.7 15.4 %all_gather.42 = f32[256,512]{1,0:T(8,128)S(1)} all-gather(f32[64,512]{1,0:T(8,128)} %bitcast.60), channel_id=1, replica_groups=mesh['x'=4,'z'=16,'y'=4,'core'=2] {'y'}, dimensions={0}, use_global_device_ids=true | all-gather | bytes 655360 | tf_op jit(solution)/shard_map/all_gather | solution.py:114
  16.1 2.2 all-gather.1
  18.3 2.2 all-gather
  20.6 0.1 pad_maximum_fusion
  20.7 5.0 %fusion = f32[4,128,896]{2,1,0:T(8,128)S(1)} fusion(f32[4,128,512]{2,1,0:T(8,128)S(1)} %bitcast.50, f32[512,896]{1,0:T(8,128)} %param.3), kind=kOutput, calls=%fused_computation | convolution fusion | flops 2818572288 | bytes 4718592 | tf_op jit(solution)/shard_map/dot_general | solution.py:14
  25.7 1.1 dynamic-slice_bitcast_fusion
  26.8 0.0 copy-start.2
  26.8 3.3 %collective-permute-start = (f32[128,896]{1,0:T(8,128)}, f32[128,896]{1,0:T(8,128)S(1)}, u32[]{:S(2)}, u32[]{:S(2)}) collective-permute-start(f32[128,896]{1,0:T(8,128)} %get-tuple-element.5), channel_id=1, source_target_pairs={{0,256},{128,384},{256,0},{384,128},{1,257},{129,385},{257,1},{385... | collective-permute-start | bytes 1376264 | tf_op jit(solution)/shard_map/ppermute | solution.py:119
  30.1 2.5 collective-permute-start.1
  32.6 4.6 %collective-permute-start.2 = (f32[128,896]{1,0:T(8,128)}, f32[128,896]{1,0:T(8,128)}, u32[]{:S(2)}, u32[]{:S(2)}) collective-permute-start(f32[128,896]{1,0:T(8,128)} %get-tuple-element.3), channel_id=1, source_target_pairs={{0,384},{128,0},{256,128},{384,256},{1,385},{129,1},{257,129},{385... | collective-permute-start | bytes 1376264 | tf_op jit(solution)/shard_map/ppermute | solution.py:119
  37.2 6.8 %collective-permute-done = f32[128,896]{1,0:T(8,128)S(1)} collective-permute-done((f32[128,896]{1,0:T(8,128)}, f32[128,896]{1,0:T(8,128)S(1)}, u32[]{:S(2)}, u32[]{:S(2)}) %collective-permute-start) | collective-permute-done | bytes 458784 | tf_op jit(solution)/shard_map/ppermute | solution.py:119
  44.0 9.1 %collective-permute-done.1 = f32[128,896]{1,0:T(8,128)} collective-permute-done((f32[128,896]{1,0:T(8,128)}, f32[128,896]{1,0:T(8,128)}, u32[]{:S(2)}, u32[]{:S(2)}) %collective-permute-start.1) | collective-permute-done | bytes 458784 | tf_op jit(solution)/shard_map/ppermute | solution.py:119
  53.0 0.0 collective-permute-done.2
  53.0 2.0 fusion.7
  55.0 13.6 %all-to-all-start.1 = ((f32[16,8,896]{2,1,0:T(8,128)}), f32[16,8,896]{2,1,0:T(8,128)S(1)}, u32[]{:S(2)}, u32[]{:S(2)}) async-start(f32[16,8,896]{2,1,0:T(8,128)} %fusion.7), calls=%async_computation.1 | async-start | bytes 917504 | tf_op jit(solution)/shard_map/all_to_all | solution.py:108
  68.6 0.0 copy-done.2
  68.6 1.1 convolution_bitcast_fusion
  69.8 0.8 copy.13
  70.6 25.1 %all-to-all-done.1 = f32[16,8,896]{2,1,0:T(8,128)S(1)} async-done(((f32[16,8,896]{2,1,0:T(8,128)}), f32[16,8,896]{2,1,0:T(8,128)S(1)}, u32[]{:S(2)}, u32[]{:S(2)}) %all-to-all-start.1) | async-done | bytes 458784 | tf_op jit(solution)/shard_map/all_to_all | solution.py:108
  95.7 9.0 %all-to-all-start = ((f32[64,1,512]{2,1,0:T(1,128)}), f32[64,1,512]{2,1,0:T(1,128)S(1)}, u32[]{:S(2)}, u32[]{:S(2)}) async-start(f32[64,1,512]{2,1,0:T(1,128)} %copy.13), calls=%async_computation | async-start | bytes 262144 | tf_op jit(solution)/shard_map/all_to_all | solution.py:108
  104.7 16.2 %all-to-all-done = f32[64,1,512]{2,1,0:T(1,128)S(1)} async-done(((f32[64,1,512]{2,1,0:T(1,128)}), f32[64,1,512]{2,1,0:T(1,128)S(1)}, u32[]{:S(2)}, u32[]{:S(2)}) %all-to-all-start) | async-done | bytes 131104 | tf_op jit(solution)/shard_map/all_to_all | solution.py:108
  120.9 0.8 broadcast_in_dim.6
  121.7 4.0 %all-to-all-start.2 = ((f32[16,8,896]{2,1,0:T(8,128)}), f32[16,8,896]{2,1,0:T(8,128)S(1)}, u32[]{:S(2)}, u32[]{:S(2)}) async-start(f32[16,8,896]{2,1,0:T(8,128)} %broadcast_in_dim.6), calls=%async_computation.2 | async-start | bytes 917504 | tf_op jit(solution)/shard_map/all_to_all | solution.py:108
  125.7 0.1 reduce_sum.18
  125.8 44.4 %all-gather.9 = f32[16,1,512]{2,1,0:T(1,128)S(1)} all-gather(f32[1,1,512]{2,1,0:T(1,128)S(1)} %bitcast.61), channel_id=4, replica_groups=mesh['x'=4,'z'=16,'y'=4,'core'=2] {'z'}, dimensions={0}, use_global_device_ids=true | all-gather | bytes 34816 | tf_op jit(solution)/shard_map/all_gather | solution.py:135
  170.2 12.0 %all-gather.3 = f32[64,1,512]{2,0,1:T(8,128)S(1)} all-gather(f32[16,1,512]{2,0,1:T(8,128)S(1)} %copy.14), channel_id=5, replica_groups=mesh['x'=4,'z'=16,'y'=4,'core'=2] {'x'}, dimensions={0}, use_global_device_ids=true | all-gather | bytes 163840 | tf_op jit(solution)/shard_map/all_gather | solution.py:136
  182.2 0.0 all-to-all-done.2
  182.2 1.3 broadcast_in_dim.15
  183.6 4.4 %all-to-all-start.3 = ((f32[4,128,896]{2,1,0:T(8,128)}), f32[4,128,896]{2,1,0:T(8,128)}, u32[]{:S(2)}, u32[]{:S(2)}) async-start(f32[4,128,896]{2,1,0:T(8,128)} %broadcast_in_dim.15), calls=%async_computation.3 | async-start | bytes 3670016 | tf_op jit(solution)/shard_map/all_to_all | solution.py:108
  188.0 12.8 %all-gather.6 = f32[256,1,512]{2,0,1:T(8,128)S(1)} all-gather(f32[64,1,512]{2,0,1:T(8,128)S(1)} %all-gather.3), channel_id=8, replica_groups=mesh['x'=4,'z'=16,'y'=4,'core'=2] {'y'}, dimensions={0}, use_global_device_ids=true | all-gather | bytes 655360 | tf_op jit(solution)/shard_map/all_gather | solution.py:137
  200.8 2.2 all-gather.7
  203.0 2.3 all-gather.8
  205.3 0.1 pad_maximum_fusion.1
  205.4 0.1 copy.15
  205.5 26.1 %shard_map.49.refs_0_ = f32[512,1024]{1,0:T(8,128)S(1)} custom-call(f32[512,512]{1,0:T(8,128)S(1)} %bitcast.49), custom_call_target="tpu_custom_call" | custom-call | flops 1610612736 | bytes 4194304 | tf_op jit(solution)/shard_map/pallas_call | solution.py:83
  231.6 26.2 %shard_map.50 = f32[512,1024]{1,0:T(8,128)S(1)} custom-call(f32[512,1024]{1,0:T(8,128)S(1)} %shard_map.49.refs_0_), custom_call_target="tpu_custom_call", output_to_operand_aliasing={{}: (0, {})} | custom-call | flops 1610612736 | bytes 4194304 | tf_op jit(solution)/shard_map/pallas_call | solution.py:83
  257.8 1.1 slice.30
  258.9 2.8 %fusion.2 = f32[512,512]{1,0:T(8,128)} fusion(f32[512,512]{1,0:T(8,128)S(1)} %bitcast.52, f32[512,1024]{1,0:T(8,128)S(1)} %shard_map.50), kind=kOutput, calls=%fused_computation.6 | convolution fusion | flops 1610612736 | bytes 3145728 | tf_op jit(solution)/shard_map/dot_general | solution.py:14
  261.7 0.0 all-to-all-done.3
  261.7 0.0 copy-start
  261.7 0.0 copy-start.1
  261.7 5.2 %fusion.4 = f32[512,896]{1,0:T(8,128)S(1)} fusion(f32[512,896]{1,0:T(8,128)} %bitcast.22, f32[512,1024]{1,0:T(8,128)S(1)} %shard_map.50), kind=kOutput, calls=%fused_computation.8 | convolution fusion | flops 2818572288 | bytes 4718592 | tf_op jit(solution)/shard_map/dot_general | solution.py:14
  266.9 0.0 copy-done
  266.9 0.0 copy-done.1
  266.9 4.8 %convolution_subtract_fusion = f32[512,896]{1,0:T(8,128)} fusion(f32[512,896]{1,0:T(8,128)S(1)} %copy-done, f32[512,512]{1,0:T(8,128)S(1)} %copy-done.1, f32[512,896]{1,0:T(8,128)S(1)} %fusion.4), kind=kOutput, calls=%fused_computation.2 | convolution fusion | flops 2819031040 | bytes 6553600 | tf_op jit(solution)/shard_map/dot_general | solution.py:14
  271.7 0.6 constant_dynamic-slice_fusion
  (6 shorter events, 0.2 us)
Async XLA Ops:
  26.8 41.8 %copy-start.2 = (f32[512,64]{0,1:T(8,128)S(1)}, f32[512,64]{0,1:T(8,128)}, u32[]{:S(2)}) copy-start(f32[512,64]{0,1:T(8,128)} %param.2) | copy-start | bytes 393220
  26.8 17.2 %collective-permute-start = (f32[128,896]{1,0:T(8,128)}, f32[128,896]{1,0:T(8,128)S(1)}, u32[]{:S(2)}, u32[]{:S(2)}) collective-permute-start(f32[128,896]{1,0:T(8,128)} %get-tuple-element.5), channel_id=1, source_target_pairs={{0,256},{128,384},{256,0},{384,128},{1,257},{129,385},{257,1},{385... | collective-permute-start | bytes 1376264 | tf_op jit(solution)/shard_map/ppermute | solution.py:119
  30.1 22.9 %collective-permute-start.1 = (f32[128,896]{1,0:T(8,128)}, f32[128,896]{1,0:T(8,128)}, u32[]{:S(2)}, u32[]{:S(2)}) collective-permute-start(f32[128,896]{1,0:T(8,128)} %get-tuple-element.4), channel_id=1, source_target_pairs={{0,128},{128,256},{256,384},{384,0},{1,129},{129,257},{257,385},{3... | collective-permute-start | bytes 1376264 | tf_op jit(solution)/shard_map/ppermute | solution.py:119
  32.6 20.4 %collective-permute-start.2 = (f32[128,896]{1,0:T(8,128)}, f32[128,896]{1,0:T(8,128)}, u32[]{:S(2)}, u32[]{:S(2)}) collective-permute-start(f32[128,896]{1,0:T(8,128)} %get-tuple-element.3), channel_id=1, source_target_pairs={{0,384},{128,0},{256,128},{384,256},{1,385},{129,1},{257,129},{385... | collective-permute-start | bytes 1376264 | tf_op jit(solution)/shard_map/ppermute | solution.py:119
  55.0 40.6 %all-to-all-start.1 = ((f32[16,8,896]{2,1,0:T(8,128)}), f32[16,8,896]{2,1,0:T(8,128)S(1)}, u32[]{:S(2)}, u32[]{:S(2)}) async-start(f32[16,8,896]{2,1,0:T(8,128)} %fusion.7), calls=%async_computation.1 | async-start | bytes 917504 | tf_op jit(solution)/shard_map/all_to_all | solution.py:108
  95.7 25.3 %all-to-all-start = ((f32[64,1,512]{2,1,0:T(1,128)}), f32[64,1,512]{2,1,0:T(1,128)S(1)}, u32[]{:S(2)}, u32[]{:S(2)}) async-start(f32[64,1,512]{2,1,0:T(1,128)} %copy.13), calls=%async_computation | async-start | bytes 262144 | tf_op jit(solution)/shard_map/all_to_all | solution.py:108
  121.7 60.5 %all-to-all-start.2 = ((f32[16,8,896]{2,1,0:T(8,128)}), f32[16,8,896]{2,1,0:T(8,128)S(1)}, u32[]{:S(2)}, u32[]{:S(2)}) async-start(f32[16,8,896]{2,1,0:T(8,128)} %broadcast_in_dim.6), calls=%async_computation.2 | async-start | bytes 917504 | tf_op jit(solution)/shard_map/all_to_all | solution.py:108
  183.6 78.2 %all-to-all-start.3 = ((f32[4,128,896]{2,1,0:T(8,128)}), f32[4,128,896]{2,1,0:T(8,128)}, u32[]{:S(2)}, u32[]{:S(2)}) async-start(f32[4,128,896]{2,1,0:T(8,128)} %broadcast_in_dim.15), calls=%async_computation.3 | async-start | bytes 3670016 | tf_op jit(solution)/shard_map/all_to_all | solution.py:108
  261.7 5.2 %copy-start = (f32[512,896]{1,0:T(8,128)S(1)}, f32[512,896]{1,0:T(8,128)}, u32[]{:S(2)}) copy-start(f32[512,896]{1,0:T(8,128)} %param.3) | copy-start | bytes 5505028
  261.7 5.2 %copy-start.1 = (f32[512,512]{1,0:T(8,128)S(1)}, f32[512,512]{1,0:T(8,128)}, u32[]{:S(2)}) copy-start(f32[512,512]{1,0:T(8,128)} %fusion.2) | copy-start | bytes 3145732

commit v3 on v2

--- a/solution.py
+++ b/solution.py
@@ -15,29 +15,50 @@
 
 
 def factor_block(s_full, rows_ref):
-    G = NB // 8
+    groups = NB // 8
     sub = lax.broadcasted_iota(jnp.int32, (8, NB), 0)
     lane = lax.broadcasted_iota(jnp.int32, (8, NB), 1)
-    s = [s_full[8 * g : 8 * g + 8, :] for g in range(G)]
-    v = [jnp.where(lane == sub + 8 * g, 1.0, 0.0).astype(jnp.float32) for g in range(G)]
-    for k in range(NB):
-        g0, i0 = k // 8, k % 8
-        col = [jnp.broadcast_to(s[g][:, k : k + 1], (8, NB)) for g in range(g0, G)]
-        r = s[g0][i0 : i0 + 1, :]
-        rows_ref[k : k + 1, :] = r
-        if k == NB - 1:
+
+    def spread(row):
+        return jnp.broadcast_to(row, (8, NB))
+
+    s = [s_full[8 * g : 8 * g + 8, :] for g in range(groups)]
+    v = [jnp.where(lane == sub + 8 * g, 1.0, 0.0).astype(jnp.float32) for g in range(groups)]
+    for g0 in range(groups):
+        at = 8 * g0
+        cols = [jnp.broadcast_to(s[g0][:, at + m : at + m + 1], (8, NB)) for m in range(8)]
+        u, w = s[g0], v[g0]
+        inv_d = jnp.zeros((8, NB), jnp.float32)
+        for j in range(8):
+            inv = spread(1.0 / cols[j][j : j + 1, :])
+            inv_d = jnp.where(sub == j, inv, inv_d)
+            if j == 7:
+                break
+            mult = jnp.where(sub > j, cols[j] * inv, 0.0)
+            for m in range(j + 1, 8):
+                cols[m] = cols[m] - mult * spread(cols[m][j : j + 1, :])
+            u = u - mult * spread(u[j : j + 1, :])
+            w = w - mult * spread(w[j : j + 1, :])
+        rows_ref[at : at + 8, :] = u
+        v[g0] = w
+        if g0 == groups - 1:
             break
-        inv = 1.0 / col[0][i0 : i0 + 1, :]
-        rd = jnp.broadcast_to(r * inv, (8, NB))
-        vd = jnp.broadcast_to(v[g0][i0 : i0 + 1, :] * inv, (8, NB))
-        for g in range(g0, G):
-            c = col[g - g0]
-            if g == g0:
-                if i0 == 7:
-                    continue
-                c = jnp.where(sub > i0, c, 0.0)
-            s[g] = s[g] - c * rd
-            v[g] = v[g] - c * vd
+        u, w = u * inv_d, w * inv_d
+        for j in range(7, 0, -1):
+            coef = jnp.where(sub < j, cols[j] * inv_d, 0.0)
+            u = u - coef * spread(u[j : j + 1, :])
+            w = w - coef * spread(w[j : j + 1, :])
+        us = [spread(u[m : m + 1, :]) for m in range(8)]
+        ws = [spread(w[m : m + 1, :]) for m in range(8)]
+        for g in range(g0 + 1, groups):
+            c = [jnp.broadcast_to(s[g][:, at + m : at + m + 1], (8, NB)) for m in range(8)]
+            du = [c[m] * us[m] for m in range(8)]
+            dw = [c[m] * ws[m] for m in range(8)]
+            while len(du) > 1:
+                du = [du[i] + du[i + 1] for i in range(0, len(du), 2)]
+                dw = [dw[i] + dw[i + 1] for i in range(0, len(dw), 2)]
+            s[g] = s[g] - du[0]
+            v[g] = v[g] - dw[0]
     return jnp.concatenate(v, axis=0)
 
 
@@ -52,7 +73,7 @@
         g_ref, a, rows = refs
         start_kernel(n, g_ref, a)
     else:
-        _, a, rows = refs
+        _, a, r_ref, x_ref, rows = refs
     sub = lax.broadcasted_iota(jnp.int32, (NB, NB), 0)
     lane = lax.broadcasted_iota(jnp.int32, (NB, NB), 1)
     wide = lax.broadcasted_iota(jnp.int32, (NB, n), 1)
@@ -74,31 +95,35 @@
         return carry
 
     lax.fori_loop(first, last, step, 0)
+    if first:
+        r_ref[...] = a[:, :n]
+        x_ref[...] = a[:, n:]
 
 
 def factor_steps(n, first, last, x):
     cost = pl.CostEstimate(
         flops=(last - first) * 2 * 6 * n * n * n // 2, bytes_accessed=4 * n * n * 4, transcendentals=0
     )
+    state = jax.ShapeDtypeStruct((n, 2 * n), jnp.float32)
+    half = jax.ShapeDtypeStruct((n, n), jnp.float32)
+    outs = (state, half, half) if first else (state,)
     return pl.pallas_call(
         functools.partial(steps_kernel, n, first, last),
-        out_shape=jax.ShapeDtypeStruct((n, 2 * n), jnp.float32),
+        out_shape=outs,
         in_specs=[pl.BlockSpec(memory_space=pltpu.VMEM)],
-        out_specs=pl.BlockSpec(memory_space=pltpu.VMEM),
+        out_specs=[pl.BlockSpec(memory_space=pltpu.VMEM)] * len(outs),
         scratch_shapes=[pltpu.VMEM((NB, NB), jnp.float32)],
-        input_output_aliases={} if first == 0 else {0: 0},
+        input_output_aliases={0: 0} if first else {},
         cost_estimate=cost,
         compiler_params=pltpu.CompilerParams(vmem_limit_bytes=32 << 20),
     )(x)
 
 
 def join_cores(part):
-    half = part.shape[0] // 2
-    both = []
-    for block in (part[:half], part[half:]):
-        pair = lax.all_gather(block, "core", axis=0, tiled=False)
-        both.append(jnp.swapaxes(pair.reshape(2, 2, 64, -1), 0, 1))
-    return jnp.concatenate(both, axis=0).reshape(2 * part.shape[0], -1)
+    other = lax.ppermute(part, "core", [(0, 1), (1, 0)])
+    first = lax.axis_index("core") == 0
+    pair = (jnp.where(first, part, other), jnp.where(first, other, part))
+    return jnp.stack(pair, axis=1).reshape(512, -1)
 
 
 CELL = ("x", "z")
@@ -111,7 +136,7 @@
 def on_device(panel_block, trailing):
     width = trailing.shape[1]
     block_t = jnp.transpose(panel_block)
-    panel_t = join_cores(lax.all_gather(block_t, "y", axis=0, tiled=True))
+    panel_t = join_cores(exchange(jnp.broadcast_to(block_t, (4, 64, 512)), "y"))
     partial = mxu(panel_t, trailing, ((1,), (0,)))
     gram = mxu(block_t, panel_t, ((1,), (1,)))
     blocks, here = partial.reshape(4, 128, width), lax.axis_index("x")
@@ -127,17 +152,16 @@
     c = (c + away[1]) + (away[0] + away[2])
     c = exchange(c.reshape(16, 8, width), "z")
     c = jnp.sum(c, axis=0)
-    c = exchange(jnp.broadcast_to(c[None], (16, 8, width)), "z")
+    c = lax.all_gather(c, "z", axis=0, tiled=True)
     c = exchange(jnp.broadcast_to(c.reshape(1, 128, width), (4, 128, width)), "x")
     c = c.reshape(512, width)
     gram = exchange(gram.reshape(64, 1, 512), CELL)
     gram = jnp.sum(gram, axis=0)
-    gram = lax.all_gather(gram, "z", axis=0, tiled=False)
-    gram = lax.all_gather(gram, "x", axis=0, tiled=False)
-    gram = join_cores(lax.all_gather(gram.reshape(64, 512), "y", axis=0, tiled=True))
-    state = factor_steps(512, 0, 2, gram)
-    state = factor_steps(512, 2, 4, state)
-    triangle, inverse = state[:, :512], state[:, 512:]
+    gram = exchange(jnp.broadcast_to(gram, (64, 1, 512)), CELL)
+    gram = lax.all_gather(gram.reshape(64, 512), "y", axis=0, tiled=False)
+    gram = join_cores(gram)
+    (state,) = factor_steps(512, 0, 2, gram)
+    _, triangle, inverse = factor_steps(512, 2, 4, state)
     basis_t = mxu(inverse, panel_t, ((1,), (0,)))
     coupling = mxu(inverse, c, ((1,), (0,)))
     projected = trailing - mxu(basis_t, coupling, ((0,), (0,)))

time: 274 us -> 198 us (0.72)
  blocking collectives: 93.5 us -> 58.6 us
  waiting for transfers between devices: 57.2 us -> 23.9 us
  Pallas kernels: 52.3 us -> 32.8 us
  starting transfers between devices: 41.3 us -> 53.2 us
    all_gather x8 -> x2, blocking collectives: 93.5 us -> 44.6 us  [the longest x1 31.3 us: on_device(): c = lax.all_gather(c, 'z', axis=0, tiled=True)]
    all_to_all x4, waiting for transfers between devices: 41.3 us -> 21.5 us  [exchange(): return lax.all_to_all(blocks, axes, 0, 0, tiled=True)]
    pallas_call x2, Pallas kernels: 52.3 us -> 32.8 us  [factor_steps(): pl.pallas_call(functools.partial(steps_kernel, n, first, last), out_shape...]
    ppermute x3, waiting for transfers between devices: 15.9 us -> 0.57 us  [on_device(): lax.ppermute(lax.dynamic_index_in_dim(blocks, (here + k) % 4, 0, False),...]
    all_to_all x0 -> x1, blocking collectives: none -> 14 us  [exchange(): return lax.all_to_all(blocks, axes, 0, 0, tiled=True)]
    all_to_all x4, starting transfers between devices: 30.9 us -> 37.3 us  [exchange(): return lax.all_to_all(blocks, axes, 0, 0, tiled=True)]
    ppermute x0 -> x2, starting transfers between devices: none -> 3.83 us  [join_cores(): other = lax.ppermute(part, 'core', [(0, 1), (1, 0)])]
  transfers between devices with their start and end apart: 7 -> 9, of which waited for: 4 -> 4; matrix products, arithmetic and copies ran while one was open for 2% -> 6% of each run, Pallas kernels for 19% -> 17%
where the time goes in v3:
time: 198 us; the launch traced here: 196 us
  blocking collectives  58.6 us (30%)
  starting transfers between devices  53.2 us (27%)
  Pallas kernels  32.8 us (17%)
  waiting for transfers between devices  23.9 us (12%)
  matrix products  18 us (9%)
  local copies, waits for them, and re-layouts  5.67 us (3%)
  other arithmetic  2.6 us (1%)
    all_to_all x4, starting transfers between devices, exchange(): return lax.all_to_all(blocks, axes, 0, 0, tiled=True)  37.3 us
    pallas_call x2, Pallas kernels, factor_steps(): pl.pallas_call(functools.partial(steps_kernel, n, first, last), out_shape...  32.8 us
    all_gather x1, blocking collectives, on_device(): c = lax.all_gather(c, 'z', axis=0, tiled=True)  31.3 us
    all_to_all x4, waiting for transfers between devices, exchange(): return lax.all_to_all(blocks, axes, 0, 0, tiled=True)  21.5 us
    dot_general x5, matrix products, mxu(): lax.dot_general(a, b, (dims, ((), ())), precision=HI, preferred_element_t...  18 us
    all_to_all x1, blocking collectives, exchange(): return lax.all_to_all(blocks, axes, 0, 0, tiled=True)  14 us
    all_gather x1, blocking collectives, on_device(): gram = lax.all_gather(gram.reshape(64, 512), 'y', axis=0, tiled=False)  13.3 us
    ppermute x3, starting transfers between devices, on_device(): lax.ppermute(lax.dynamic_index_in_dim(blocks, (here + k) % 4, 0, False),...  12.1 us
  transfers between devices with their start and end apart: 9, of which 4 were waited for; matrix products, arithmetic and copies ran while one was open for 6% of the time, Pallas kernels for 17%

profile of v3, /device:TPU:24, one launch (start us, length us, event | category | flops | bytes accessed | tf_op | source)
XLA Modules:
  0.0 195.6 jit_solution(6454647395560899582)
XLA Ops:
  0.6 1.0 broadcast_in_dim.11
  1.6 14.0 %all_to_all.25 = f32[4,64,512]{2,1,0:T(8,128)S(1)} all-to-all(f32[4,64,512]{2,1,0:T(8,128)S(1)} %broadcast_in_dim.11), channel_id=1, replica_groups=mesh['x'=4,'z'=16,'y'=4,'core'=2] {'y'}, dimensions={0} | all-to-all | bytes 1048576 | tf_op jit(solution)/shard_map/all_to_all | solution.py:133
  15.6 1.9 collective-permute-start
  17.5 0.0 copy-start.1
  17.5 1.8 collective-permute-done
  19.4 0.1 select_bitcast_fusion.3
  19.5 0.1 pad_maximum_fusion
  19.6 0.0 copy-done.1
  19.6 1.1 convolution_bitcast_fusion
  20.8 0.8 copy.14
  21.6 16.5 %all-to-all-start.1 = ((f32[64,1,512]{2,1,0:T(1,128)}), f32[64,1,512]{2,1,0:T(1,128)S(1)}, u32[]{:S(2)}, u32[]{:S(2)}) async-start(f32[64,1,512]{2,1,0:T(1,128)} %copy.14), calls=%async_computation.1 | async-start | bytes 262144 | tf_op jit(solution)/shard_map/all_to_all | solution.py:133
  38.0 5.0 %fusion = f32[4,128,896]{2,1,0:T(8,128)S(1)} fusion(f32[4,128,512]{2,1,0:T(8,128)S(1)} %bitcast.48, f32[512,896]{1,0:T(8,128)} %param.3), kind=kOutput, calls=%fused_computation | convolution fusion | flops 2818572288 | bytes 4718592 | tf_op jit(solution)/shard_map/dot_general | solution.py:14
  43.1 1.1 dynamic-slice_bitcast_fusion
  44.2 5.1 %collective-permute-start.2 = (f32[128,896]{1,0:T(8,128)}, f32[128,896]{1,0:T(8,128)S(1)}, u32[]{:S(2)}, u32[]{:S(2)}) collective-permute-start(f32[128,896]{1,0:T(8,128)} %get-tuple-element.9), channel_id=1, source_target_pairs={{0,256},{128,384},{256,0},{384,128},{1,257},{129,385},{257,1},{385... | collective-permute-start | bytes 1376264 | tf_op jit(solution)/shard_map/ppermute | solution.py:144
  49.3 2.6 %collective-permute-start.3 = (f32[128,896]{1,0:T(8,128)}, f32[128,896]{1,0:T(8,128)}, u32[]{:S(2)}, u32[]{:S(2)}) collective-permute-start(f32[128,896]{1,0:T(8,128)} %get-tuple-element.8), channel_id=1, source_target_pairs={{0,128},{128,256},{256,384},{384,0},{1,129},{129,257},{257,385},{3... | collective-permute-start | bytes 1376264 | tf_op jit(solution)/shard_map/ppermute | solution.py:144
  51.9 4.5 %collective-permute-start.4 = (f32[128,896]{1,0:T(8,128)}, f32[128,896]{1,0:T(8,128)}, u32[]{:S(2)}, u32[]{:S(2)}) collective-permute-start(f32[128,896]{1,0:T(8,128)} %get-tuple-element.7), channel_id=1, source_target_pairs={{0,384},{128,0},{256,128},{384,256},{1,385},{129,1},{257,129},{385... | collective-permute-start | bytes 1376264 | tf_op jit(solution)/shard_map/ppermute | solution.py:144
  56.4 0.0 all-to-all-done.1
  56.4 0.1 reduce_sum.18
  56.5 0.7 broadcast_in_dim.12
  57.2 12.5 %all-to-all-start.2 = ((f32[64,1,512]{2,1,0:T(1,128)}), f32[64,1,512]{2,1,0:T(1,128)S(1)}, u32[]{:S(2)}, u32[]{:S(2)}) async-start(f32[64,1,512]{2,1,0:T(1,128)} %broadcast_in_dim.12), calls=%async_computation.2 | async-start | bytes 262144 | tf_op jit(solution)/shard_map/all_to_all | solution.py:133
  69.7 0.0 collective-permute-done.2
  69.7 0.6 collective-permute-done.3
  70.3 0.0 collective-permute-done.4
  70.3 2.0 %fusion.3 = f32[16,8,896]{2,1,0:T(8,128)} fusion(f32[128,896]{1,0:T(8,128)S(1)} %collective-permute-done.2, f32[128,896]{1,0:T(8,128)} %collective-permute-done.3, f32[128,896]{1,0:T(8,128)} %collective-permute-done.4, f32[4,128,896]{2,1,0:T(8,128)S(1)} %fusion, s32[]{:T(128)S(6)} %select_n.56), kind=kLoop, calls=%fused_computation.12 | loop fusion | flops 344064 | bytes 2293764 | tf_op jit(solution)/shard_map/reshape | solution.py:153
  72.3 12.8 %all-to-all-done.2 = f32[64,1,512]{2,1,0:T(1,128)S(1)} async-done(((f32[64,1,512]{2,1,0:T(1,128)}), f32[64,1,512]{2,1,0:T(1,128)S(1)}, u32[]{:S(2)}, u32[]{:S(2)}) %all-to-all-start.2) | async-done | bytes 131104 | tf_op jit(solution)/shard_map/all_to_all | solution.py:133
  85.1 3.7 %all-to-all-start.3 = ((f32[16,8,896]{2,1,0:T(8,128)}), f32[16,8,896]{2,1,0:T(8,128)S(1)}, u32[]{:S(2)}, u32[]{:S(2)}) async-start(f32[16,8,896]{2,1,0:T(8,128)} %fusion.3), calls=%async_computation.3 | async-start | bytes 917504 | tf_op jit(solution)/shard_map/all_to_all | solution.py:133
  88.8 13.3 %all-gather = f32[256,1,512]{2,1,0:T(1,128)S(1)} all-gather(f32[64,1,512]{2,1,0:T(1,128)S(1)} %all-to-all-done.2), channel_id=2, replica_groups=mesh['x'=4,'z'=16,'y'=4,'core'=2] {'y'}, dimensions={0}, use_global_device_ids=true | all-gather | bytes 655360 | tf_op jit(solution)/shard_map/all_gather | solution.py:161
  102.1 1.9 collective-permute-start.1
  104.1 8.7 %all-to-all-done.3 = f32[16,8,896]{2,1,0:T(8,128)S(1)} async-done(((f32[16,8,896]{2,1,0:T(8,128)}), f32[16,8,896]{2,1,0:T(8,128)S(1)}, u32[]{:S(2)}, u32[]{:S(2)}) %all-to-all-start.3) | async-done | bytes 458784 | tf_op jit(solution)/shard_map/all_to_all | solution.py:133
  112.8 31.3 %all_gather.7 = f32[128,896]{1,0:T(8,128)S(1)} all-gather(f32[8,896]{1,0:T(8,128)S(1)} %reduce_sum.19), channel_id=1, replica_groups=mesh['x'=4,'z'=16,'y'=4,'core'=2] {'z'}, dimensions={0}, use_global_device_ids=true | all-gather | bytes 487424 | tf_op jit(solution)/shard_map/all_gather | solution.py:155
  144.1 1.3 broadcast_in_dim.13
  145.5 4.6 %all-to-all-start.4 = ((f32[4,128,896]{2,1,0:T(8,128)}), f32[4,128,896]{2,1,0:T(8,128)}, u32[]{:S(2)}, u32[]{:S(2)}) async-start(f32[4,128,896]{2,1,0:T(8,128)} %broadcast_in_dim.13), calls=%async_computation.4 | async-start | bytes 3670016 | tf_op jit(solution)/shard_map/all_to_all | solution.py:133
  150.1 0.0 collective-permute-done.1
  150.1 0.1 select_bitcast_fusion.1
  150.2 0.1 pad_maximum_fusion.1
  150.3 0.1 copy.15
  150.4 15.8 %shard_map.49.refs_0_ = f32[512,1024]{1,0:T(8,128)S(1)} custom-call(f32[512,512]{1,0:T(8,128)S(1)} %bitcast.46), custom_call_target="tpu_custom_call" | custom-call | flops 1610612736 | bytes 4194304 | tf_op jit(solution)/shard_map/pallas_call | solution.py:110
  166.1 17.0 %shard_map.50 = (f32[512,1024]{1,0:T(8,128)S(1)}, f32[512,512]{1,0:T(8,128)}, f32[512,512]{1,0:T(8,128)S(1)}) custom-call(f32[512,1024]{1,0:T(8,128)S(1)} %shard_map.49.refs_0_), custom_call_target="tpu_custom_call", output_to_operand_aliasing={{0}: (0, {})} | custom-call | flops 1610612736 | bytes 4194304 | tf_op jit(solution)/shard_map/pallas_call | solution.py:110
  183.1 1.8 fusion.5
  185.0 0.0 all-to-all-done.4
  185.0 0.0 copy-start
  185.0 5.2 %fusion.4 = f32[512,896]{1,0:T(8,128)S(1)} fusion(f32[512,512]{1,0:T(8,128)S(1)} %get-tuple-element.6, f32[512,896]{1,0:T(8,128)} %bitcast.17), kind=kOutput, calls=%fused_computation.17 | convolution fusion | flops 2818572288 | bytes 4718592 | tf_op jit(solution)/shard_map/dot_general | solution.py:14
  190.2 0.6 constant_dynamic-slice_fusion
  190.8 0.0 copy-done
  190.8 4.8 %convolution_subtract_fusion = f32[512,896]{1,0:T(8,128)} fusion(f32[512,896]{1,0:T(8,128)S(1)} %copy-done, f32[512,512]{1,0:T(8,128)S(1)} %fusion.5, f32[512,896]{1,0:T(8,128)S(1)} %fusion.4), kind=kOutput, calls=%fused_computation.2 | convolution fusion | flops 2819031040 | bytes 6553600 | tf_op jit(solution)/shard_map/dot_general | solution.py:14
  (2 shorter events, 0.1 us)
Async XLA Ops:
  15.6 3.8 %collective-permute-start = (f32[4,64,512]{2,1,0:T(8,128)S(1)}, f32[4,64,512]{2,1,0:T(8,128)S(1)}, u32[]{:S(2)}, u32[]{:S(2)}) collective-permute-start(f32[4,64,512]{2,1,0:T(8,128)S(1)} %all_to_all.25), channel_id=1, source_target_pairs={{0,1},{1,0},{2,3},{3,2},{4,5},{5,4},{6,7},{7,6},{8,9},{9,8},{10,11... | collective-permute-start | bytes 1572872 | tf_op jit(solution)/shard_map/ppermute | solution.py:123
  17.5 2.1 %copy-start.1 = (f32[512,64]{0,1:T(8,128)S(1)}, f32[512,64]{0,1:T(8,128)}, u32[]{:S(2)}) copy-start(f32[512,64]{0,1:T(8,128)} %param.2) | copy-start | bytes 393220
  21.6 34.8 %all-to-all-start.1 = ((f32[64,1,512]{2,1,0:T(1,128)}), f32[64,1,512]{2,1,0:T(1,128)S(1)}, u32[]{:S(2)}, u32[]{:S(2)}) async-start(f32[64,1,512]{2,1,0:T(1,128)} %copy.14), calls=%async_computation.1 | async-start | bytes 262144 | tf_op jit(solution)/shard_map/all_to_all | solution.py:133
  44.2 25.5 %collective-permute-start.2 = (f32[128,896]{1,0:T(8,128)}, f32[128,896]{1,0:T(8,128)S(1)}, u32[]{:S(2)}, u32[]{:S(2)}) collective-permute-start(f32[128,896]{1,0:T(8,128)} %get-tuple-element.9), channel_id=1, source_target_pairs={{0,256},{128,384},{256,0},{384,128},{1,257},{129,385},{257,1},{385... | collective-permute-start | bytes 1376264 | tf_op jit(solution)/shard_map/ppermute | solution.py:144
  49.3 21.0 %collective-permute-start.3 = (f32[128,896]{1,0:T(8,128)}, f32[128,896]{1,0:T(8,128)}, u32[]{:S(2)}, u32[]{:S(2)}) collective-permute-start(f32[128,896]{1,0:T(8,128)} %get-tuple-element.8), channel_id=1, source_target_pairs={{0,128},{128,256},{256,384},{384,0},{1,129},{129,257},{257,385},{3... | collective-permute-start | bytes 1376264 | tf_op jit(solution)/shard_map/ppermute | solution.py:144
  51.9 18.4 %collective-permute-start.4 = (f32[128,896]{1,0:T(8,128)}, f32[128,896]{1,0:T(8,128)}, u32[]{:S(2)}, u32[]{:S(2)}) collective-permute-start(f32[128,896]{1,0:T(8,128)} %get-tuple-element.7), channel_id=1, source_target_pairs={{0,384},{128,0},{256,128},{384,256},{1,385},{129,1},{257,129},{385... | collective-permute-start | bytes 1376264 | tf_op jit(solution)/shard_map/ppermute | solution.py:144
  57.2 27.9 %all-to-all-start.2 = ((f32[64,1,512]{2,1,0:T(1,128)}), f32[64,1,512]{2,1,0:T(1,128)S(1)}, u32[]{:S(2)}, u32[]{:S(2)}) async-start(f32[64,1,512]{2,1,0:T(1,128)} %broadcast_in_dim.12), calls=%async_computation.2 | async-start | bytes 262144 | tf_op jit(solution)/shard_map/all_to_all | solution.py:133
  85.1 27.7 %all-to-all-start.3 = ((f32[16,8,896]{2,1,0:T(8,128)}), f32[16,8,896]{2,1,0:T(8,128)S(1)}, u32[]{:S(2)}, u32[]{:S(2)}) async-start(f32[16,8,896]{2,1,0:T(8,128)} %fusion.3), calls=%async_computation.3 | async-start | bytes 917504 | tf_op jit(solution)/shard_map/all_to_all | solution.py:133
  102.1 47.9 %collective-permute-start.1 = (f32[4,64,512]{2,1,0:T(8,128)S(1)}, f32[4,64,512]{2,1,0:T(8,128)S(1)}, u32[]{:S(2)}, u32[]{:S(2)}) collective-permute-start(f32[4,64,512]{2,1,0:T(8,128)S(1)} %bitcast.50), channel_id=1, source_target_pairs={{0,1},{1,0},{2,3},{3,2},{4,5},{5,4},{6,7},{7,6},{8,9},{9,8},{10,11... | collective-permute-start | bytes 1572872 | tf_op jit(solution)/shard_map/ppermute | solution.py:123
  145.5 39.5 %all-to-all-start.4 = ((f32[4,128,896]{2,1,0:T(8,128)}), f32[4,128,896]{2,1,0:T(8,128)}, u32[]{:S(2)}, u32[]{:S(2)}) async-start(f32[4,128,896]{2,1,0:T(8,128)} %broadcast_in_dim.13), calls=%async_computation.4 | async-start | bytes 3670016 | tf_op jit(solution)/shard_map/all_to_all | solution.py:133
  185.0 5.8 %copy-start = (f32[512,896]{1,0:T(8,128)S(1)}, f32[512,896]{1,0:T(8,128)}, u32[]{:S(2)}) copy-start(f32[512,896]{1,0:T(8,128)} %param.3) | copy-start | bytes 5505028

commit v4 on v3

--- a/solution.py
+++ b/solution.py
@@ -10,8 +10,8 @@
 NB = 128
 
 
-def mxu(a, b, dims):
-    return lax.dot_general(a, b, (dims, ((), ())), precision=HI, preferred_element_type=jnp.float32)
+def mxu(a, b, dims, precision=HI):
+    return lax.dot_general(a, b, (dims, ((), ())), precision=precision, preferred_element_type=jnp.float32)
 
 
 def factor_block(s_full, rows_ref):
@@ -152,19 +152,22 @@
     c = (c + away[1]) + (away[0] + away[2])
     c = exchange(c.reshape(16, 8, width), "z")
     c = jnp.sum(c, axis=0)
-    c = lax.all_gather(c, "z", axis=0, tiled=True)
+    c = exchange(jnp.broadcast_to(c, (16, 8, width)), "z")
     c = exchange(jnp.broadcast_to(c.reshape(1, 128, width), (4, 128, width)), "x")
     c = c.reshape(512, width)
-    gram = exchange(gram.reshape(64, 1, 512), CELL)
+    gram = exchange(gram.reshape(4, 16, 512), "x")
     gram = jnp.sum(gram, axis=0)
-    gram = exchange(jnp.broadcast_to(gram, (64, 1, 512)), CELL)
+    gram = exchange(gram.reshape(16, 1, 512), "z")
+    gram = jnp.sum(gram, axis=0)
+    gram = exchange(jnp.broadcast_to(gram, (16, 1, 512)), "z")
+    gram = exchange(jnp.broadcast_to(gram.reshape(1, 16, 512), (4, 16, 512)), "x")
     gram = lax.all_gather(gram.reshape(64, 512), "y", axis=0, tiled=False)
     gram = join_cores(gram)
     (state,) = factor_steps(512, 0, 2, gram)
     _, triangle, inverse = factor_steps(512, 2, 4, state)
     basis_t = mxu(inverse, panel_t, ((1,), (0,)))
     coupling = mxu(inverse, c, ((1,), (0,)))
-    projected = trailing - mxu(basis_t, coupling, ((0,), (0,)))
+    projected = trailing - mxu(basis_t, coupling, ((0,), (0,)), lax.Precision.HIGH)
     row = 128 * lax.axis_index("x") + 8 * lax.axis_index("z")
     mine = lax.dynamic_slice_in_dim(coupling, row, 8, axis=0)
     return (triangle, mine, projected)

time: 198 us -> 216 us (1.091)
  waiting for transfers between devices: 23.9 us -> 62.1 us
  blocking collectives: 58.6 us -> 43.1 us
  starting transfers between devices: 53.2 us -> 49.9 us
  matrix products: 18 us -> 14.9 us
    all_to_all x4 -> x6, waiting for transfers between devices: 21.5 us -> 60.3 us  [exchange(): return lax.all_to_all(blocks, axes, 0, 0, tiled=True)]
    all_gather x1 -> x0, blocking collectives: 31.3 us -> none  [on_device(): c = lax.all_gather(c, 'z', axis=0, tiled=True)]
    all_to_all x1 -> x2, blocking collectives: 14 us -> 30.3 us  [exchange(): return lax.all_to_all(blocks, axes, 0, 0, tiled=True)]
    dot_general x5, matrix products: 18 us -> 14.9 us  [mxu(): lax.dot_general(a, b, (dims, ((), ())), precision=precision, preferred_el...]
    ppermute x3, starting transfers between devices: 12.1 us -> 9.9 us  [on_device(): lax.ppermute(lax.dynamic_index_in_dim(blocks, (here + k) % 4, 0, False),...]
    all_to_all x4 -> x6, starting transfers between devices: 37.3 us -> 36.2 us  [exchange(): return lax.all_to_all(blocks, axes, 0, 0, tiled=True)]
  transfers between devices with their start and end apart: 9 -> 11, of which waited for: 4 -> 6; matrix products, arithmetic and copies ran while one was open for 6% -> 4% of each run, Pallas kernels for 17% -> 15%
where the time goes in v4:
time: 216 us; the launch traced here: 213 us
  waiting for transfers between devices  62.1 us (29%)
  starting transfers between devices  49.9 us (23%)
  blocking collectives  43.1 us (20%)
  Pallas kernels  32.8 us (15%)
  matrix products  14.9 us (7%)
  local copies, waits for them, and re-layouts  6.83 us (3%)
  other arithmetic  2.54 us (1%)
    all_to_all x6, waiting for transfers between devices, exchange(): return lax.all_to_all(blocks, axes, 0, 0, tiled=True)  60.3 us
    all_to_all x6, starting transfers between devices, exchange(): return lax.all_to_all(blocks, axes, 0, 0, tiled=True)  36.2 us
    pallas_call x2, Pallas kernels, factor_steps(): pl.pallas_call(functools.partial(steps_kernel, n, first, last), out_shape...  32.8 us
    all_to_all x2, blocking collectives, exchange(): return lax.all_to_all(blocks, axes, 0, 0, tiled=True)  30.3 us
    dot_general x5, matrix products, mxu(): lax.dot_general(a, b, (dims, ((), ())), precision=precision, preferred_el...  14.9 us
    all_gather x1, blocking collectives, on_device(): gram = lax.all_gather(gram.reshape(64, 512), 'y', axis=0, tiled=False)  12.8 us
    ppermute x3, starting transfers between devices, on_device(): lax.ppermute(lax.dynamic_index_in_dim(blocks, (here + k) % 4, 0, False),...  9.9 us
  transfers between devices with their start and end apart: 11, of which 6 were waited for; matrix products, arithmetic and copies ran while one was open for 4% of the time, Pallas kernels for 15%

profile of v4, /device:TPU:24, one launch (start us, length us, event | category | flops | bytes accessed | tf_op | source)
XLA Modules:
  0.0 213.1 jit_solution(9793732912066134450)
XLA Ops:
  0.6 1.0 broadcast_in_dim.23
  1.6 14.0 %all_to_all.40 = f32[4,64,512]{2,1,0:T(8,128)S(1)} all-to-all(f32[4,64,512]{2,1,0:T(8,128)S(1)} %broadcast_in_dim.23), channel_id=1, replica_groups=mesh['x'=4,'z'=16,'y'=4,'core'=2] {'y'}, dimensions={0} | all-to-all | bytes 1048576 | tf_op jit(solution)/shard_map/all_to_all | solution.py:133
  15.6 1.9 collective-permute-start
  17.5 0.0 copy-start
  17.5 1.8 collective-permute-done
  19.4 0.1 select_bitcast_fusion.3
  19.5 0.1 pad_maximum_fusion
  19.6 0.0 copy-done
  19.6 3.5 %fusion = f32[4,128,896]{2,1,0:T(8,128)S(1)} fusion(f32[4,128,512]{2,1,0:T(8,128)S(1)} %bitcast.50, f32[512,896]{1,0:T(8,128)S(1)} %copy-done), kind=kOutput, calls=%fused_computation | convolution fusion | flops 2818572288 | bytes 4718592 | tf_op jit(solution)/shard_map/dot_general | solution.py:14
  23.2 0.0 copy-start.2
  23.2 1.1 dynamic-slice_bitcast_fusion
  24.3 2.8 %collective-permute-start.2 = (f32[128,896]{1,0:T(8,128)}, f32[128,896]{1,0:T(8,128)S(1)}, u32[]{:S(2)}, u32[]{:S(2)}) collective-permute-start(f32[128,896]{1,0:T(8,128)} %get-tuple-element.9), channel_id=1, source_target_pairs={{0,256},{128,384},{256,0},{384,128},{1,257},{129,385},{257,1},{385... | collective-permute-start | bytes 1376264 | tf_op jit(solution)/shard_map/ppermute | solution.py:144
  27.1 2.5 %collective-permute-start.3 = (f32[128,896]{1,0:T(8,128)}, f32[128,896]{1,0:T(8,128)}, u32[]{:S(2)}, u32[]{:S(2)}) collective-permute-start(f32[128,896]{1,0:T(8,128)} %get-tuple-element.8), channel_id=1, source_target_pairs={{0,128},{128,256},{256,384},{384,0},{1,129},{129,257},{257,385},{3... | collective-permute-start | bytes 1376264 | tf_op jit(solution)/shard_map/ppermute | solution.py:144
  29.7 4.6 %collective-permute-start.4 = (f32[128,896]{1,0:T(8,128)}, f32[128,896]{1,0:T(8,128)}, u32[]{:S(2)}, u32[]{:S(2)}) collective-permute-start(f32[128,896]{1,0:T(8,128)} %get-tuple-element.7), channel_id=1, source_target_pairs={{0,384},{128,0},{256,128},{384,256},{1,385},{129,1},{257,129},{385... | collective-permute-start | bytes 1376264 | tf_op jit(solution)/shard_map/ppermute | solution.py:144
  34.2 0.0 copy-done.2
  34.2 1.1 fusion.4
  35.4 16.4 %all_to_all.41 = f32[4,16,512]{2,1,0:T(8,128)S(1)} all-to-all(f32[4,16,512]{2,1,0:T(8,128)S(1)} %bitcast.56), channel_id=1, replica_groups=mesh['x'=4,'z'=16,'y'=4,'core'=2] {'x'}, dimensions={0} | all-to-all | bytes 262144 | tf_op jit(solution)/shard_map/all_to_all | solution.py:133
  51.8 0.6 reshape.36
  52.4 13.1 %all-to-all-start.2 = ((f32[16,1,512]{2,1,0:T(1,128)}), f32[16,1,512]{2,1,0:T(1,128)S(1)}, u32[]{:S(2)}, u32[]{:S(2)}) async-start(f32[16,1,512]{2,1,0:T(1,128)} %reshape.36), calls=%async_computation.2 | async-start | bytes 65536 | tf_op jit(solution)/shard_map/all_to_all | solution.py:133
  65.5 12.6 %all-to-all-done.2 = f32[16,1,512]{2,1,0:T(1,128)S(1)} async-done(((f32[16,1,512]{2,1,0:T(1,128)}), f32[16,1,512]{2,1,0:T(1,128)S(1)}, u32[]{:S(2)}, u32[]{:S(2)}) %all-to-all-start.2) | async-done | bytes 32800 | tf_op jit(solution)/shard_map/all_to_all | solution.py:133
  78.1 0.6 broadcast_in_dim.24
  78.8 3.5 %all-to-all-start.3 = ((f32[16,1,512]{2,1,0:T(1,128)}), f32[16,1,512]{2,1,0:T(1,128)S(1)}, u32[]{:S(2)}, u32[]{:S(2)}) async-start(f32[16,1,512]{2,1,0:T(1,128)} %broadcast_in_dim.24), calls=%async_computation.3 | async-start | bytes 65536 | tf_op jit(solution)/shard_map/all_to_all | solution.py:133
  82.3 0.0 collective-permute-done.2
  82.3 0.0 collective-permute-done.3
  82.3 0.0 collective-permute-done.4
  82.3 2.0 fusion.3
  84.3 10.5 %all-to-all-done.3 = f32[16,1,512]{2,1,0:T(1,128)S(1)} async-done(((f32[16,1,512]{2,1,0:T(1,128)}), f32[16,1,512]{2,1,0:T(1,128)S(1)}, u32[]{:S(2)}, u32[]{:S(2)}) %all-to-all-start.3) | async-done | bytes 32800 | tf_op jit(solution)/shard_map/all_to_all | solution.py:133
  94.8 3.6 %all-to-all-start.5 = ((f32[16,8,896]{2,1,0:T(8,128)}), f32[16,8,896]{2,1,0:T(8,128)S(1)}, u32[]{:S(2)}, u32[]{:S(2)}) async-start(f32[16,8,896]{2,1,0:T(8,128)} %fusion.3), calls=%async_computation.5 | async-start | bytes 917504 | tf_op jit(solution)/shard_map/all_to_all | solution.py:133
  98.4 22.9 %all-to-all-done.5 = f32[16,8,896]{2,1,0:T(8,128)S(1)} async-done(((f32[16,8,896]{2,1,0:T(8,128)}), f32[16,8,896]{2,1,0:T(8,128)S(1)}, u32[]{:S(2)}, u32[]{:S(2)}) %all-to-all-start.5) | async-done | bytes 458784 | tf_op jit(solution)/shard_map/all_to_all | solution.py:133
  121.3 0.7 broadcast_in_dim.26
  122.0 4.3 %all-to-all-start.4 = ((f32[4,16,512]{2,1,0:T(8,128)}), f32[4,16,512]{2,1,0:T(8,128)S(1)}, u32[]{:S(2)}, u32[]{:S(2)}) async-start(f32[4,16,512]{2,1,0:T(8,128)} %broadcast_in_dim.26), calls=%async_computation.4 | async-start | bytes 262144 | tf_op jit(solution)/shard_map/all_to_all | solution.py:133
  126.3 5.9 %all-to-all-done.4 = f32[4,16,512]{2,1,0:T(8,128)S(1)} async-done(((f32[4,16,512]{2,1,0:T(8,128)}), f32[4,16,512]{2,1,0:T(8,128)S(1)}, u32[]{:S(2)}, u32[]{:S(2)}) %all-to-all-start.4) | async-done | bytes 131104 | tf_op jit(solution)/shard_map/all_to_all | solution.py:133
  132.2 0.8 broadcast_in_dim.27
  133.0 7.2 %all-to-all-start.6 = ((f32[16,8,896]{2,1,0:T(8,128)}), f32[16,8,896]{2,1,0:T(8,128)S(1)}, u32[]{:S(2)}, u32[]{:S(2)}) async-start(f32[16,8,896]{2,1,0:T(8,128)} %broadcast_in_dim.27), calls=%async_computation.6 | async-start | bytes 917504 | tf_op jit(solution)/shard_map/all_to_all | solution.py:133
  140.2 12.8 %all_gather.3 = f32[4,64,512]{2,1,0:T(8,128)S(1)} all-gather(f32[1,64,512]{2,1,0:T(8,128)S(1)} %bitcast.55), channel_id=1, replica_groups=mesh['x'=4,'z'=16,'y'=4,'core'=2] {'y'}, dimensions={0}, use_global_device_ids=true | all-gather | bytes 655360 | tf_op jit(solution)/shard_map/all_gather | solution.py:164
  153.0 1.9 collective-permute-start.1
  154.9 8.3 %all-to-all-done.6 = f32[16,8,896]{2,1,0:T(8,128)S(1)} async-done(((f32[16,8,896]{2,1,0:T(8,128)}), f32[16,8,896]{2,1,0:T(8,128)S(1)}, u32[]{:S(2)}, u32[]{:S(2)}) %all-to-all-start.6) | async-done | bytes 458784 | tf_op jit(solution)/shard_map/all_to_all | solution.py:133
  163.2 1.3 broadcast_in_dim.29
  164.5 4.6 %all-to-all-start.7 = ((f32[4,128,896]{2,1,0:T(8,128)}), f32[4,128,896]{2,1,0:T(8,128)}, u32[]{:S(2)}, u32[]{:S(2)}) async-start(f32[4,128,896]{2,1,0:T(8,128)} %broadcast_in_dim.29), calls=%async_computation.7 | async-start | bytes 3670016 | tf_op jit(solution)/shard_map/all_to_all | solution.py:133
  169.1 0.0 collective-permute-done.1
  169.1 0.1 select_bitcast_fusion.1
  169.3 0.1 pad_maximum_fusion.1
  169.4 0.1 copy.11
  169.4 15.8 %shard_map.49.refs_0_ = f32[512,1024]{1,0:T(8,128)S(1)} custom-call(f32[512,512]{1,0:T(8,128)S(1)} %bitcast.49), custom_call_target="tpu_custom_call" | custom-call | flops 1610612736 | bytes 4194304 | tf_op jit(solution)/shard_map/pallas_call | solution.py:110
  185.2 17.0 %shard_map.50 = (f32[512,1024]{1,0:T(8,128)S(1)}, f32[512,512]{1,0:T(8,128)}, f32[512,512]{1,0:T(8,128)S(1)}) custom-call(f32[512,1024]{1,0:T(8,128)S(1)} %shard_map.49.refs_0_), custom_call_target="tpu_custom_call", output_to_operand_aliasing={{0}: (0, {})} | custom-call | flops 1610612736 | bytes 4194304 | tf_op jit(solution)/shard_map/pallas_call | solution.py:110
  202.2 1.8 fusion.6
  204.1 0.0 all-to-all-done.7
  204.1 0.0 copy-start.1
  204.1 5.2 %fusion.5 = f32[512,896]{1,0:T(8,128)S(1)} fusion(f32[512,512]{1,0:T(8,128)S(1)} %get-tuple-element.6, f32[512,896]{1,0:T(8,128)} %bitcast.19), kind=kOutput, calls=%fused_computation.18 | convolution fusion | flops 2818572288 | bytes 4718592 | tf_op jit(solution)/shard_map/dot_general | solution.py:14
  209.3 0.6 constant_dynamic-slice_fusion
  209.9 0.0 copy-done.1
  209.9 3.2 %convolution_subtract_fusion = f32[512,896]{1,0:T(8,128)} fusion(f32[512,896]{1,0:T(8,128)S(1)} %copy-done.1, f32[512,512]{1,0:T(8,128)S(1)} %fusion.6, f32[512,896]{1,0:T(8,128)S(1)} %fusion.5), kind=kOutput, calls=%fused_computation.2 | convolution fusion | flops 1409744896 | bytes 6553600 | tf_op jit(solution)/shard_map/dot_general | solution.py:14
  (4 shorter events, 0.1 us)
Async XLA Ops:
  15.6 3.8 %collective-permute-start = (f32[4,64,512]{2,1,0:T(8,128)S(1)}, f32[4,64,512]{2,1,0:T(8,128)S(1)}, u32[]{:S(2)}, u32[]{:S(2)}) collective-permute-start(f32[4,64,512]{2,1,0:T(8,128)S(1)} %all_to_all.40), channel_id=1, source_target_pairs={{0,1},{1,0},{2,3},{3,2},{4,5},{5,4},{6,7},{7,6},{8,9},{9,8},{10,11... | collective-permute-start | bytes 1572872 | tf_op jit(solution)/shard_map/ppermute | solution.py:123
  17.5 2.1 copy-start
  23.2 11.0 %copy-start.2 = (f32[512,64]{0,1:T(8,128)S(1)}, f32[512,64]{0,1:T(8,128)}, u32[]{:S(2)}) copy-start(f32[512,64]{0,1:T(8,128)} %param.2) | copy-start | bytes 393220
  24.3 58.0 %collective-permute-start.2 = (f32[128,896]{1,0:T(8,128)}, f32[128,896]{1,0:T(8,128)S(1)}, u32[]{:S(2)}, u32[]{:S(2)}) collective-permute-start(f32[128,896]{1,0:T(8,128)} %get-tuple-element.9), channel_id=1, source_target_pairs={{0,256},{128,384},{256,0},{384,128},{1,257},{129,385},{257,1},{385... | collective-permute-start | bytes 1376264 | tf_op jit(solution)/shard_map/ppermute | solution.py:144
  27.1 55.1 %collective-permute-start.3 = (f32[128,896]{1,0:T(8,128)}, f32[128,896]{1,0:T(8,128)}, u32[]{:S(2)}, u32[]{:S(2)}) collective-permute-start(f32[128,896]{1,0:T(8,128)} %get-tuple-element.8), channel_id=1, source_target_pairs={{0,128},{128,256},{256,384},{384,0},{1,129},{129,257},{257,385},{3... | collective-permute-start | bytes 1376264 | tf_op jit(solution)/shard_map/ppermute | solution.py:144
  29.7 52.6 %collective-permute-start.4 = (f32[128,896]{1,0:T(8,128)}, f32[128,896]{1,0:T(8,128)}, u32[]{:S(2)}, u32[]{:S(2)}) collective-permute-start(f32[128,896]{1,0:T(8,128)} %get-tuple-element.7), channel_id=1, source_target_pairs={{0,384},{128,0},{256,128},{384,256},{1,385},{129,1},{257,129},{385... | collective-permute-start | bytes 1376264 | tf_op jit(solution)/shard_map/ppermute | solution.py:144
  52.4 25.7 %all-to-all-start.2 = ((f32[16,1,512]{2,1,0:T(1,128)}), f32[16,1,512]{2,1,0:T(1,128)S(1)}, u32[]{:S(2)}, u32[]{:S(2)}) async-start(f32[16,1,512]{2,1,0:T(1,128)} %reshape.36), calls=%async_computation.2 | async-start | bytes 65536 | tf_op jit(solution)/shard_map/all_to_all | solution.py:133
  78.8 16.1 %all-to-all-start.3 = ((f32[16,1,512]{2,1,0:T(1,128)}), f32[16,1,512]{2,1,0:T(1,128)S(1)}, u32[]{:S(2)}, u32[]{:S(2)}) async-start(f32[16,1,512]{2,1,0:T(1,128)} %broadcast_in_dim.24), calls=%async_computation.3 | async-start | bytes 65536 | tf_op jit(solution)/shard_map/all_to_all | solution.py:133
  94.8 26.5 %all-to-all-start.5 = ((f32[16,8,896]{2,1,0:T(8,128)}), f32[16,8,896]{2,1,0:T(8,128)S(1)}, u32[]{:S(2)}, u32[]{:S(2)}) async-start(f32[16,8,896]{2,1,0:T(8,128)} %fusion.3), calls=%async_computation.5 | async-start | bytes 917504 | tf_op jit(solution)/shard_map/all_to_all | solution.py:133
  122.0 10.3 %all-to-all-start.4 = ((f32[4,16,512]{2,1,0:T(8,128)}), f32[4,16,512]{2,1,0:T(8,128)S(1)}, u32[]{:S(2)}, u32[]{:S(2)}) async-start(f32[4,16,512]{2,1,0:T(8,128)} %broadcast_in_dim.26), calls=%async_computation.4 | async-start | bytes 262144 | tf_op jit(solution)/shard_map/all_to_all | solution.py:133
  133.0 30.2 %all-to-all-start.6 = ((f32[16,8,896]{2,1,0:T(8,128)}), f32[16,8,896]{2,1,0:T(8,128)S(1)}, u32[]{:S(2)}, u32[]{:S(2)}) async-start(f32[16,8,896]{2,1,0:T(8,128)} %broadcast_in_dim.27), calls=%async_computation.6 | async-start | bytes 917504 | tf_op jit(solution)/shard_map/all_to_all | solution.py:133
  153.0 16.1 %collective-permute-start.1 = (f32[4,64,512]{2,1,0:T(8,128)S(1)}, f32[4,64,512]{2,1,0:T(8,128)S(1)}, u32[]{:S(2)}, u32[]{:S(2)}) collective-permute-start(f32[4,64,512]{2,1,0:T(8,128)S(1)} %all_gather.3), channel_id=1, source_target_pairs={{0,1},{1,0},{2,3},{3,2},{4,5},{5,4},{6,7},{7,6},{8,9},{9,8},{10,11... | collective-permute-start | bytes 1572872 | tf_op jit(solution)/shard_map/ppermute | solution.py:123
  164.5 39.5 %all-to-all-start.7 = ((f32[4,128,896]{2,1,0:T(8,128)}), f32[4,128,896]{2,1,0:T(8,128)}, u32[]{:S(2)}, u32[]{:S(2)}) async-start(f32[4,128,896]{2,1,0:T(8,128)} %broadcast_in_dim.29), calls=%async_computation.7 | async-start | bytes 3670016 | tf_op jit(solution)/shard_map/all_to_all | solution.py:133
  204.1 5.8 %copy-start.1 = (f32[512,896]{1,0:T(8,128)S(1)}, f32[512,896]{1,0:T(8,128)}, u32[]{:S(2)}) copy-start(f32[512,896]{1,0:T(8,128)} %param.3) | copy-start | bytes 5505028

commit v5 on v3

--- a/solution.py
+++ b/solution.py
@@ -10,8 +10,8 @@
 NB = 128
 
 
-def mxu(a, b, dims):
-    return lax.dot_general(a, b, (dims, ((), ())), precision=HI, preferred_element_type=jnp.float32)
+def mxu(a, b, dims, precision=HI):
+    return lax.dot_general(a, b, (dims, ((), ())), precision=precision, preferred_element_type=jnp.float32)
 
 
 def factor_block(s_full, rows_ref):
@@ -62,36 +62,42 @@
     return jnp.concatenate(v, axis=0)
 
 
-def start_kernel(n, g_ref, a_ref):
-    a_ref[:, :n] = g_ref[...]
-    row = lax.broadcasted_iota(jnp.int32, (n, n), 0)
-    a_ref[:, n:] = jnp.where(row == lax.broadcasted_iota(jnp.int32, (n, n), 1), 1.0, 0.0)
+def block_row(n, c, a, linv):
+    at, to = c * NB, (c + 1) * NB
+    upper = lax.broadcasted_iota(jnp.int32, (NB, NB), 0) <= lax.broadcasted_iota(jnp.int32, (NB, NB), 1)
+    right = mxu(linv, a[at:to, at:n], ((1,), (0,)))
+    left = [mxu(linv, a[at:to, n : n + at], ((1,), (0,)))] if c else []
+    if to < n:
+        below = mxu(a[to:n, at:to], linv, ((1,), (1,)))
+        a[to:n, to:n] -= mxu(below, right[:, NB:], ((1,), (0,)))
+        if c:
+            a[to:n, n : n + at] -= mxu(below, left[0], ((1,), (0,)))
+        a[to:n, n + at : n + to] = -mxu(below, linv, ((1,), (0,)))
+        a[at:to, to:n] = right[:, NB:]
+        a[at:to, n + to : 2 * n] = jnp.zeros((NB, n - to), jnp.float32)
+    if c:
+        a[at:to, :at] = jnp.zeros((NB, at), jnp.float32)
+        a[at:to, n : n + at] = left[0]
+    a[at:to, at:to] = jnp.where(upper, right[:, :NB], 0.0)
+    a[at:to, n + at : n + to] = linv
 
 
 def steps_kernel(n, first, last, *refs):
     if first == 0:
         g_ref, a, rows = refs
-        start_kernel(n, g_ref, a)
+        a[:, :n] = g_ref[...]
     else:
         _, a, r_ref, x_ref, rows = refs
     sub = lax.broadcasted_iota(jnp.int32, (NB, NB), 0)
     lane = lax.broadcasted_iota(jnp.int32, (NB, NB), 1)
-    wide = lax.broadcasted_iota(jnp.int32, (NB, n), 1)
-    high = lax.broadcasted_iota(jnp.int32, (NB, n), 0)
-    tall = lax.broadcasted_iota(jnp.int32, (n, n), 0)
 
     def step(kb, carry):
         at = pl.multiple_of(kb * NB, NB)
         v = factor_block(a[pl.ds(at, NB), pl.ds(at, NB)], rows)
-        rt = rows[...]
-        d = jnp.sum(jnp.where(sub == lane, rt, 0.0), axis=1, keepdims=True)
-        linv = v * lax.rsqrt(d)
-        out = mxu(linv, a[pl.ds(at, NB), :], ((1,), (0,)))
-        rm = jnp.where(wide >= at + NB, out[:, :n], 0.0)
-        full = jnp.concatenate([rm, out[:, n:]], axis=1)
-        a[...] -= mxu(rm, full, ((0,), (0,)))
-        a[pl.ds(at, NB), n:] = out[:, n:]
-        a[pl.ds(at, NB), :n] = jnp.where(wide >= at + high, out[:, :n], 0.0)
+        d = jnp.sum(jnp.where(sub == lane, rows[...], 0.0), axis=1, keepdims=True)
+        rows[...] = v * lax.rsqrt(d)
+        for c in range(first, last):
+            pl.when(kb == c)(lambda c=c: block_row(n, c, a, rows[...]))
         return carry
 
     lax.fori_loop(first, last, step, 0)
@@ -115,7 +121,7 @@
         scratch_shapes=[pltpu.VMEM((NB, NB), jnp.float32)],
         input_output_aliases={0: 0} if first else {},
         cost_estimate=cost,
-        compiler_params=pltpu.CompilerParams(vmem_limit_bytes=32 << 20),
+        compiler_params=pltpu.CompilerParams(vmem_limit_bytes=16 << 20),
     )(x)
 
 
@@ -164,7 +170,7 @@
     _, triangle, inverse = factor_steps(512, 2, 4, state)
     basis_t = mxu(inverse, panel_t, ((1,), (0,)))
     coupling = mxu(inverse, c, ((1,), (0,)))
-    projected = trailing - mxu(basis_t, coupling, ((0,), (0,)))
+    projected = trailing - mxu(basis_t, coupling, ((0,), (0,)), lax.Precision.HIGH)
     row = 128 * lax.axis_index("x") + 8 * lax.axis_index("z")
     mine = lax.dynamic_slice_in_dim(coupling, row, 8, axis=0)
     return (triangle, mine, projected)

time: 198 us -> 191 us (0.965)
  Pallas kernels: 32.8 us -> 26.7 us
    pallas_call x2, Pallas kernels: 32.8 us -> 26.7 us  [factor_steps(): pl.pallas_call(functools.partial(steps_kernel, n, first, last), out_shape...]
  transfers between devices with their start and end apart: 9 -> 9, of which waited for: 4 -> 4; matrix products, arithmetic and copies ran while one was open for 6% -> 7% of each run, Pallas kernels for 17% -> 14%
where the time goes in v5:
time: 191 us; the launch traced here: 188 us
  blocking collectives  58.6 us (31%)
  starting transfers between devices  53.2 us (28%)
  Pallas kernels  26.7 us (14%)
  waiting for transfers between devices  23.9 us (13%)
  matrix products  16.4 us (9%)
  local copies, waits for them, and re-layouts  5.67 us (3%)
  other arithmetic  2.6 us (1%)
    all_to_all x4, starting transfers between devices, exchange(): return lax.all_to_all(blocks, axes, 0, 0, tiled=True)  37.3 us
    all_gather x1, blocking collectives, on_device(): c = lax.all_gather(c, 'z', axis=0, tiled=True)  31.3 us
    pallas_call x2, Pallas kernels, factor_steps(): pl.pallas_call(functools.partial(steps_kernel, n, first, last), out_shape...  26.7 us
    all_to_all x4, waiting for transfers between devices, exchange(): return lax.all_to_all(blocks, axes, 0, 0, tiled=True)  21.5 us
    dot_general x5, matrix products, mxu(): lax.dot_general(a, b, (dims, ((), ())), precision=precision, preferred_el...  16.4 us
    all_to_all x1, blocking collectives, exchange(): return lax.all_to_all(blocks, axes, 0, 0, tiled=True)  14 us
    all_gather x1, blocking collectives, on_device(): gram = lax.all_gather(gram.reshape(64, 512), 'y', axis=0, tiled=False)  13.3 us
    ppermute x3, starting transfers between devices, on_device(): lax.ppermute(lax.dynamic_index_in_dim(blocks, (here + k) % 4, 0, False),...  12.1 us
  transfers between devices with their start and end apart: 9, of which 4 were waited for; matrix products, arithmetic and copies ran while one was open for 7% of the time, Pallas kernels for 14%

profile of v5, /device:TPU:24, one launch (start us, length us, event | category | flops | bytes accessed | tf_op | source)
XLA Modules:
  0.0 187.9 jit_solution(2841312451141357453)
XLA Ops:
  0.6 1.0 broadcast_in_dim.11
  1.6 14.0 %all_to_all.25 = f32[4,64,512]{2,1,0:T(8,128)S(1)} all-to-all(f32[4,64,512]{2,1,0:T(8,128)S(1)} %broadcast_in_dim.11), channel_id=1, replica_groups=mesh['x'=4,'z'=16,'y'=4,'core'=2] {'y'}, dimensions={0} | all-to-all | bytes 1048576 | tf_op jit(solution)/shard_map/all_to_all | solution.py:139
  15.6 1.9 %collective-permute-start = (f32[4,64,512]{2,1,0:T(8,128)S(1)}, f32[4,64,512]{2,1,0:T(8,128)S(1)}, u32[]{:S(2)}, u32[]{:S(2)}) collective-permute-start(f32[4,64,512]{2,1,0:T(8,128)S(1)} %all_to_all.25), channel_id=1, source_target_pairs={{0,1},{1,0},{2,3},{3,2},{4,5},{5,4},{6,7},{7,6},{8,9},{9,8},{10,11... | collective-permute-start | bytes 1572872 | tf_op jit(solution)/shard_map/ppermute | solution.py:129
  17.5 0.0 copy-start.1
  17.5 1.8 collective-permute-done
  19.4 0.1 select_bitcast_fusion.3
  19.5 0.1 pad_maximum_fusion
  19.6 0.0 copy-done.1
  19.6 1.1 convolution_bitcast_fusion
  20.8 0.8 copy.14
  21.6 16.5 %all-to-all-start.1 = ((f32[64,1,512]{2,1,0:T(1,128)}), f32[64,1,512]{2,1,0:T(1,128)S(1)}, u32[]{:S(2)}, u32[]{:S(2)}) async-start(f32[64,1,512]{2,1,0:T(1,128)} %copy.14), calls=%async_computation.1 | async-start | bytes 262144 | tf_op jit(solution)/shard_map/all_to_all | solution.py:139
  38.0 5.0 %fusion = f32[4,128,896]{2,1,0:T(8,128)S(1)} fusion(f32[4,128,512]{2,1,0:T(8,128)S(1)} %bitcast.48, f32[512,896]{1,0:T(8,128)} %param.3), kind=kOutput, calls=%fused_computation | convolution fusion | flops 2818572288 | bytes 4718592 | tf_op jit(solution)/shard_map/dot_general | solution.py:14
  43.1 1.1 dynamic-slice_bitcast_fusion
  44.2 5.1 %collective-permute-start.2 = (f32[128,896]{1,0:T(8,128)}, f32[128,896]{1,0:T(8,128)S(1)}, u32[]{:S(2)}, u32[]{:S(2)}) collective-permute-start(f32[128,896]{1,0:T(8,128)} %get-tuple-element.9), channel_id=1, source_target_pairs={{0,256},{128,384},{256,0},{384,128},{1,257},{129,385},{257,1},{385... | collective-permute-start | bytes 1376264 | tf_op jit(solution)/shard_map/ppermute | solution.py:150
  49.3 2.6 %collective-permute-start.3 = (f32[128,896]{1,0:T(8,128)}, f32[128,896]{1,0:T(8,128)}, u32[]{:S(2)}, u32[]{:S(2)}) collective-permute-start(f32[128,896]{1,0:T(8,128)} %get-tuple-element.8), channel_id=1, source_target_pairs={{0,128},{128,256},{256,384},{384,0},{1,129},{129,257},{257,385},{3... | collective-permute-start | bytes 1376264 | tf_op jit(solution)/shard_map/ppermute | solution.py:150
  51.9 4.5 %collective-permute-start.4 = (f32[128,896]{1,0:T(8,128)}, f32[128,896]{1,0:T(8,128)}, u32[]{:S(2)}, u32[]{:S(2)}) collective-permute-start(f32[128,896]{1,0:T(8,128)} %get-tuple-element.7), channel_id=1, source_target_pairs={{0,384},{128,0},{256,128},{384,256},{1,385},{129,1},{257,129},{385... | collective-permute-start | bytes 1376264 | tf_op jit(solution)/shard_map/ppermute | solution.py:150
  56.4 0.0 all-to-all-done.1
  56.4 0.1 reduce_sum.18
  56.5 0.7 broadcast_in_dim.12
  57.2 12.5 %all-to-all-start.2 = ((f32[64,1,512]{2,1,0:T(1,128)}), f32[64,1,512]{2,1,0:T(1,128)S(1)}, u32[]{:S(2)}, u32[]{:S(2)}) async-start(f32[64,1,512]{2,1,0:T(1,128)} %broadcast_in_dim.12), calls=%async_computation.2 | async-start | bytes 262144 | tf_op jit(solution)/shard_map/all_to_all | solution.py:139
  69.7 0.0 collective-permute-done.2
  69.7 0.6 collective-permute-done.3
  70.3 0.0 collective-permute-done.4
  70.3 2.0 %fusion.3 = f32[16,8,896]{2,1,0:T(8,128)} fusion(f32[128,896]{1,0:T(8,128)S(1)} %collective-permute-done.2, f32[128,896]{1,0:T(8,128)} %collective-permute-done.3, f32[128,896]{1,0:T(8,128)} %collective-permute-done.4, f32[4,128,896]{2,1,0:T(8,128)S(1)} %fusion, s32[]{:T(128)S(6)} %select_n.56), kind=kLoop, calls=%fused_computation.12 | loop fusion | flops 344064 | bytes 2293764 | tf_op jit(solution)/shard_map/reshape | solution.py:159
  72.3 12.8 %all-to-all-done.2 = f32[64,1,512]{2,1,0:T(1,128)S(1)} async-done(((f32[64,1,512]{2,1,0:T(1,128)}), f32[64,1,512]{2,1,0:T(1,128)S(1)}, u32[]{:S(2)}, u32[]{:S(2)}) %all-to-all-start.2) | async-done | bytes 131104 | tf_op jit(solution)/shard_map/all_to_all | solution.py:139
  85.1 3.7 %all-to-all-start.3 = ((f32[16,8,896]{2,1,0:T(8,128)}), f32[16,8,896]{2,1,0:T(8,128)S(1)}, u32[]{:S(2)}, u32[]{:S(2)}) async-start(f32[16,8,896]{2,1,0:T(8,128)} %fusion.3), calls=%async_computation.3 | async-start | bytes 917504 | tf_op jit(solution)/shard_map/all_to_all | solution.py:139
  88.8 13.3 %all-gather = f32[256,1,512]{2,1,0:T(1,128)S(1)} all-gather(f32[64,1,512]{2,1,0:T(1,128)S(1)} %all-to-all-done.2), channel_id=2, replica_groups=mesh['x'=4,'z'=16,'y'=4,'core'=2] {'y'}, dimensions={0}, use_global_device_ids=true | all-gather | bytes 655360 | tf_op jit(solution)/shard_map/all_gather | solution.py:167
  102.1 1.9 %collective-permute-start.1 = (f32[4,64,512]{2,1,0:T(8,128)S(1)}, f32[4,64,512]{2,1,0:T(8,128)S(1)}, u32[]{:S(2)}, u32[]{:S(2)}) collective-permute-start(f32[4,64,512]{2,1,0:T(8,128)S(1)} %bitcast.50), channel_id=1, source_target_pairs={{0,1},{1,0},{2,3},{3,2},{4,5},{5,4},{6,7},{7,6},{8,9},{9,8},{10,11... | collective-permute-start | bytes 1572872 | tf_op jit(solution)/shard_map/ppermute | solution.py:129
  104.1 8.7 %all-to-all-done.3 = f32[16,8,896]{2,1,0:T(8,128)S(1)} async-done(((f32[16,8,896]{2,1,0:T(8,128)}), f32[16,8,896]{2,1,0:T(8,128)S(1)}, u32[]{:S(2)}, u32[]{:S(2)}) %all-to-all-start.3) | async-done | bytes 458784 | tf_op jit(solution)/shard_map/all_to_all | solution.py:139
  112.8 31.3 %all_gather.7 = f32[128,896]{1,0:T(8,128)S(1)} all-gather(f32[8,896]{1,0:T(8,128)S(1)} %reduce_sum.19), channel_id=1, replica_groups=mesh['x'=4,'z'=16,'y'=4,'core'=2] {'z'}, dimensions={0}, use_global_device_ids=true | all-gather | bytes 487424 | tf_op jit(solution)/shard_map/all_gather | solution.py:161
  144.1 1.3 broadcast_in_dim.13
  145.5 4.6 %all-to-all-start.4 = ((f32[4,128,896]{2,1,0:T(8,128)}), f32[4,128,896]{2,1,0:T(8,128)}, u32[]{:S(2)}, u32[]{:S(2)}) async-start(f32[4,128,896]{2,1,0:T(8,128)} %broadcast_in_dim.13), calls=%async_computation.4 | async-start | bytes 3670016 | tf_op jit(solution)/shard_map/all_to_all | solution.py:139
  150.1 0.0 collective-permute-done.1
  150.1 0.1 select_bitcast_fusion.1
  150.2 0.1 pad_maximum_fusion.1
  150.3 0.1 copy.15
  150.4 13.1 %shard_map.49.refs_0_ = f32[512,1024]{1,0:T(8,128)S(1)} custom-call(f32[512,512]{1,0:T(8,128)S(1)} %bitcast.46), custom_call_target="tpu_custom_call" | custom-call | flops 1610612736 | bytes 4194304 | tf_op jit(solution)/shard_map/pallas_call | solution.py:116
  163.5 13.5 %shard_map.50 = (f32[512,1024]{1,0:T(8,128)S(1)}, f32[512,512]{1,0:T(8,128)}, f32[512,512]{1,0:T(8,128)S(1)}) custom-call(f32[512,1024]{1,0:T(8,128)S(1)} %shard_map.49.refs_0_), custom_call_target="tpu_custom_call", output_to_operand_aliasing={{0}: (0, {})} | custom-call | flops 1610612736 | bytes 4194304 | tf_op jit(solution)/shard_map/pallas_call | solution.py:116
  177.0 1.8 fusion.5
  178.9 0.0 all-to-all-done.4
  178.9 0.0 copy-start
  178.9 5.2 %fusion.4 = f32[512,896]{1,0:T(8,128)S(1)} fusion(f32[512,512]{1,0:T(8,128)S(1)} %get-tuple-element.6, f32[512,896]{1,0:T(8,128)} %bitcast.17), kind=kOutput, calls=%fused_computation.17 | convolution fusion | flops 2818572288 | bytes 4718592 | tf_op jit(solution)/shard_map/dot_general | solution.py:14
  184.1 0.6 constant_dynamic-slice_fusion
  184.7 0.0 copy-done
  184.7 3.2 %convolution_subtract_fusion = f32[512,896]{1,0:T(8,128)} fusion(f32[512,896]{1,0:T(8,128)S(1)} %copy-done, f32[512,512]{1,0:T(8,128)S(1)} %fusion.5, f32[512,896]{1,0:T(8,128)S(1)} %fusion.4), kind=kOutput, calls=%fused_computation.2 | convolution fusion | flops 1409744896 | bytes 6553600 | tf_op jit(solution)/shard_map/dot_general | solution.py:14
  (2 shorter events, 0.1 us)
Async XLA Ops:
  15.6 3.8 %collective-permute-start = (f32[4,64,512]{2,1,0:T(8,128)S(1)}, f32[4,64,512]{2,1,0:T(8,128)S(1)}, u32[]{:S(2)}, u32[]{:S(2)}) collective-permute-start(f32[4,64,512]{2,1,0:T(8,128)S(1)} %all_to_all.25), channel_id=1, source_target_pairs={{0,1},{1,0},{2,3},{3,2},{4,5},{5,4},{6,7},{7,6},{8,9},{9,8},{10,11... | collective-permute-start | bytes 1572872 | tf_op jit(solution)/shard_map/ppermute | solution.py:129
  17.5 2.1 %copy-start.1 = (f32[512,64]{0,1:T(8,128)S(1)}, f32[512,64]{0,1:T(8,128)}, u32[]{:S(2)}) copy-start(f32[512,64]{0,1:T(8,128)} %param.2) | copy-start | bytes 393220
  21.6 34.8 %all-to-all-start.1 = ((f32[64,1,512]{2,1,0:T(1,128)}), f32[64,1,512]{2,1,0:T(1,128)S(1)}, u32[]{:S(2)}, u32[]{:S(2)}) async-start(f32[64,1,512]{2,1,0:T(1,128)} %copy.14), calls=%async_computation.1 | async-start | bytes 262144 | tf_op jit(solution)/shard_map/all_to_all | solution.py:139
  44.2 25.5 %collective-permute-start.2 = (f32[128,896]{1,0:T(8,128)}, f32[128,896]{1,0:T(8,128)S(1)}, u32[]{:S(2)}, u32[]{:S(2)}) collective-permute-start(f32[128,896]{1,0:T(8,128)} %get-tuple-element.9), channel_id=1, source_target_pairs={{0,256},{128,384},{256,0},{384,128},{1,257},{129,385},{257,1},{385... | collective-permute-start | bytes 1376264 | tf_op jit(solution)/shard_map/ppermute | solution.py:150
  49.3 21.0 %collective-permute-start.3 = (f32[128,896]{1,0:T(8,128)}, f32[128,896]{1,0:T(8,128)}, u32[]{:S(2)}, u32[]{:S(2)}) collective-permute-start(f32[128,896]{1,0:T(8,128)} %get-tuple-element.8), channel_id=1, source_target_pairs={{0,128},{128,256},{256,384},{384,0},{1,129},{129,257},{257,385},{3... | collective-permute-start | bytes 1376264 | tf_op jit(solution)/shard_map/ppermute | solution.py:150
  51.9 18.4 %collective-permute-start.4 = (f32[128,896]{1,0:T(8,128)}, f32[128,896]{1,0:T(8,128)}, u32[]{:S(2)}, u32[]{:S(2)}) collective-permute-start(f32[128,896]{1,0:T(8,128)} %get-tuple-element.7), channel_id=1, source_target_pairs={{0,384},{128,0},{256,128},{384,256},{1,385},{129,1},{257,129},{385... | collective-permute-start | bytes 1376264 | tf_op jit(solution)/shard_map/ppermute | solution.py:150
  57.2 27.9 %all-to-all-start.2 = ((f32[64,1,512]{2,1,0:T(1,128)}), f32[64,1,512]{2,1,0:T(1,128)S(1)}, u32[]{:S(2)}, u32[]{:S(2)}) async-start(f32[64,1,512]{2,1,0:T(1,128)} %broadcast_in_dim.12), calls=%async_computation.2 | async-start | bytes 262144 | tf_op jit(solution)/shard_map/all_to_all | solution.py:139
  85.1 27.7 %all-to-all-start.3 = ((f32[16,8,896]{2,1,0:T(8,128)}), f32[16,8,896]{2,1,0:T(8,128)S(1)}, u32[]{:S(2)}, u32[]{:S(2)}) async-start(f32[16,8,896]{2,1,0:T(8,128)} %fusion.3), calls=%async_computation.3 | async-start | bytes 917504 | tf_op jit(solution)/shard_map/all_to_all | solution.py:139
  102.1 47.9 %collective-permute-start.1 = (f32[4,64,512]{2,1,0:T(8,128)S(1)}, f32[4,64,512]{2,1,0:T(8,128)S(1)}, u32[]{:S(2)}, u32[]{:S(2)}) collective-permute-start(f32[4,64,512]{2,1,0:T(8,128)S(1)} %bitcast.50), channel_id=1, source_target_pairs={{0,1},{1,0},{2,3},{3,2},{4,5},{5,4},{6,7},{7,6},{8,9},{9,8},{10,11... | collective-permute-start | bytes 1572872 | tf_op jit(solution)/shard_map/ppermute | solution.py:129
  145.5 33.4 %all-to-all-start.4 = ((f32[4,128,896]{2,1,0:T(8,128)}), f32[4,128,896]{2,1,0:T(8,128)}, u32[]{:S(2)}, u32[]{:S(2)}) async-start(f32[4,128,896]{2,1,0:T(8,128)} %broadcast_in_dim.13), calls=%async_computation.4 | async-start | bytes 3670016 | tf_op jit(solution)/shard_map/all_to_all | solution.py:139
  178.9 5.8 %copy-start = (f32[512,896]{1,0:T(8,128)S(1)}, f32[512,896]{1,0:T(8,128)}, u32[]{:S(2)}) copy-start(f32[512,896]{1,0:T(8,128)} %param.3) | copy-start | bytes 5505028

commit v6 on v5

--- a/solution.py
+++ b/solution.py
@@ -87,7 +87,11 @@
         g_ref, a, rows = refs
         a[:, :n] = g_ref[...]
     else:
-        _, a, r_ref, x_ref, rows = refs
+        a_in, r_ref, x_ref, a, rows = refs
+        done = first * NB
+        r_ref[:done, :] = a_in[:done, :n]
+        x_ref[:done, :] = a_in[:done, n:]
+        a[done:, :] = a_in[done:, :]
     sub = lax.broadcasted_iota(jnp.int32, (NB, NB), 0)
     lane = lax.broadcasted_iota(jnp.int32, (NB, NB), 1)
 
@@ -102,8 +106,8 @@
 
     lax.fori_loop(first, last, step, 0)
     if first:
-        r_ref[...] = a[:, :n]
-        x_ref[...] = a[:, n:]
+        r_ref[done:, :] = a[done:, :n]
+        x_ref[done:, :] = a[done:, n:]
 
 
 def factor_steps(n, first, last, x):
@@ -112,14 +116,14 @@
     )
     state = jax.ShapeDtypeStruct((n, 2 * n), jnp.float32)
     half = jax.ShapeDtypeStruct((n, n), jnp.float32)
-    outs = (state, half, half) if first else (state,)
+    outs = (half, half) if first else (state,)
+    held = [pltpu.VMEM((n, 2 * n), jnp.float32)] if first else []
     return pl.pallas_call(
         functools.partial(steps_kernel, n, first, last),
         out_shape=outs,
         in_specs=[pl.BlockSpec(memory_space=pltpu.VMEM)],
         out_specs=[pl.BlockSpec(memory_space=pltpu.VMEM)] * len(outs),
-        scratch_shapes=[pltpu.VMEM((NB, NB), jnp.float32)],
-        input_output_aliases={0: 0} if first else {},
+        scratch_shapes=held + [pltpu.VMEM((NB, NB), jnp.float32)],
         cost_estimate=cost,
         compiler_params=pltpu.CompilerParams(vmem_limit_bytes=16 << 20),
     )(x)
@@ -145,17 +149,17 @@
     panel_t = join_cores(exchange(jnp.broadcast_to(block_t, (4, 64, 512)), "y"))
     partial = mxu(panel_t, trailing, ((1,), (0,)))
     gram = mxu(block_t, panel_t, ((1,), (1,)))
+    gram, partial = lax.optimization_barrier((gram, partial))
     blocks, here = partial.reshape(4, 128, width), lax.axis_index("x")
-    away = [
-        lax.ppermute(
+    away = {}
+    for k in (2, 3, 1):
+        away[k] = lax.ppermute(
             lax.dynamic_index_in_dim(blocks, (here + k) % 4, 0, False),
             "x",
             [(i, (i + k) % 4) for i in range(4)],
         )
-        for k in (1, 2, 3)
-    ]
     c = lax.dynamic_index_in_dim(blocks, here, 0, False)
-    c = (c + away[1]) + (away[0] + away[2])
+    c = (c + away[2]) + (away[1] + away[3])
     c = exchange(c.reshape(16, 8, width), "z")
     c = jnp.sum(c, axis=0)
     c = lax.all_gather(c, "z", axis=0, tiled=True)
@@ -167,7 +171,7 @@
     gram = lax.all_gather(gram.reshape(64, 512), "y", axis=0, tiled=False)
     gram = join_cores(gram)
     (state,) = factor_steps(512, 0, 2, gram)
-    _, triangle, inverse = factor_steps(512, 2, 4, state)
+    triangle, inverse = factor_steps(512, 2, 4, state)
     basis_t = mxu(inverse, panel_t, ((1,), (0,)))
     coupling = mxu(inverse, c, ((1,), (0,)))
     projected = trailing - mxu(basis_t, coupling, ((0,), (0,)), lax.Precision.HIGH)

time: 191 us -> 190 us (level)
  waiting for transfers between devices: 23.9 us -> 26.7 us
  starting transfers between devices: 53.2 us -> 50.5 us
    all_to_all x4, starting transfers between devices: 37.3 us -> 34.5 us  [exchange(): return lax.all_to_all(blocks, axes, 0, 0, tiled=True)]
    all_to_all x4, waiting for transfers between devices: 21.5 us -> 23.5 us  [exchange(): return lax.all_to_all(blocks, axes, 0, 0, tiled=True)]
  transfers between devices with their start and end apart: 9 -> 9, of which waited for: 4 -> 5; matrix products, arithmetic and copies ran while one was open for 7% -> 4% of each run, Pallas kernels for 14% -> 14%
where the time goes in v6:
time: 190 us; the launch traced here: 187 us
  blocking collectives  58.6 us (31%)
  starting transfers between devices  50.5 us (27%)
  waiting for transfers between devices  26.7 us (14%)
  Pallas kernels  26.7 us (14%)
  matrix products  14.9 us (8%)
  local copies, waits for them, and re-layouts  5.93 us (3%)
  other arithmetic  2.55 us (1%)
    all_to_all x4, starting transfers between devices, exchange(): return lax.all_to_all(blocks, axes, 0, 0, tiled=True)  34.5 us
    all_gather x1, blocking collectives, on_device(): c = lax.all_gather(c, 'z', axis=0, tiled=True)  31.3 us
    pallas_call x2, Pallas kernels, factor_steps(): pl.pallas_call(functools.partial(steps_kernel, n, first, last), out_shape...  26.7 us
    all_to_all x4, waiting for transfers between devices, exchange(): return lax.all_to_all(blocks, axes, 0, 0, tiled=True)  23.5 us
    dot_general x5, matrix products, mxu(): lax.dot_general(a, b, (dims, ((), ())), precision=precision, preferred_el...  14.9 us
    all_to_all x1, blocking collectives, exchange(): return lax.all_to_all(blocks, axes, 0, 0, tiled=True)  14 us
    all_gather x1, blocking collectives, on_device(): gram = lax.all_gather(gram.reshape(64, 512), 'y', axis=0, tiled=False)  13.3 us
    ppermute x3, starting transfers between devices, on_device(): lax.ppermute(lax.dynamic_index_in_dim(blocks, (here + k) % 4, 0, False),...  12.1 us
  transfers between devices with their start and end apart: 9, of which 5 were waited for; matrix products, arithmetic and copies ran while one was open for 4% of the time, Pallas kernels for 14%

profile of v6, /device:TPU:24, one launch (start us, length us, event | category | flops | bytes accessed | tf_op | source)
XLA Modules:
  0.0 186.7 jit_solution(17663200615716874293)
XLA Ops:
  0.6 1.0 broadcast_in_dim.11
  1.6 14.0 %all_to_all.25 = f32[4,64,512]{2,1,0:T(8,128)S(1)} all-to-all(f32[4,64,512]{2,1,0:T(8,128)S(1)} %broadcast_in_dim.11), channel_id=1, replica_groups=mesh['x'=4,'z'=16,'y'=4,'core'=2] {'y'}, dimensions={0} | all-to-all | bytes 1048576 | tf_op jit(solution)/shard_map/all_to_all | solution.py:143
  15.6 1.9 %collective-permute-start = (f32[4,64,512]{2,1,0:T(8,128)S(1)}, f32[4,64,512]{2,1,0:T(8,128)S(1)}, u32[]{:S(2)}, u32[]{:S(2)}) collective-permute-start(f32[4,64,512]{2,1,0:T(8,128)S(1)} %all_to_all.25), channel_id=1, source_target_pairs={{0,1},{1,0},{2,3},{3,2},{4,5},{5,4},{6,7},{7,6},{8,9},{9,8},{10,11... | collective-permute-start | bytes 1572872 | tf_op jit(solution)/shard_map/ppermute | solution.py:133
  17.5 0.0 copy-start.2
  17.5 1.9 collective-permute-done
  19.4 0.1 select_bitcast_fusion.3
  19.5 0.0 copy-start
  19.5 0.1 pad_maximum_fusion
  19.6 0.0 copy-done.2
  19.6 1.1 convolution_bitcast_fusion
  20.7 0.3 copy-done
  21.0 3.5 %fusion.2 = f32[512,896]{1,0:T(8,128)S(1)} fusion(f32[512,512]{1,0:T(8,128)S(1)} %bitcast.45, f32[512,896]{1,0:T(8,128)S(1)} %copy-done), kind=kOutput, calls=%fused_computation.15 | convolution fusion | flops 2818572288 | bytes 4718592 | tf_op jit(solution)/shard_map/dot_general | solution.py:14
  24.5 0.8 copy.12
  25.3 16.5 %all-to-all-start.1 = ((f32[64,1,512]{2,1,0:T(1,128)}), f32[64,1,512]{2,1,0:T(1,128)S(1)}, u32[]{:S(2)}, u32[]{:S(2)}) async-start(f32[64,1,512]{2,1,0:T(1,128)} %copy.12), calls=%async_computation.1 | async-start | bytes 262144 | tf_op jit(solution)/shard_map/all_to_all | solution.py:143
  41.9 1.1 dynamic-slice_bitcast_fusion
  43.0 5.1 %collective-permute-start.2 = (f32[128,896]{1,0:T(8,128)}, f32[128,896]{1,0:T(8,128)S(1)}, u32[]{:S(2)}, u32[]{:S(2)}) collective-permute-start(f32[128,896]{1,0:T(8,128)} %get-tuple-element.13), channel_id=1, source_target_pairs={{0,256},{128,384},{256,0},{384,128},{1,257},{129,385},{257,1},{385... | collective-permute-start | bytes 1376264 | tf_op jit(solution)/shard_map/ppermute | solution.py:156
  48.1 2.6 %collective-permute-start.3 = (f32[128,896]{1,0:T(8,128)}, f32[128,896]{1,0:T(8,128)}, u32[]{:S(2)}, u32[]{:S(2)}) collective-permute-start(f32[128,896]{1,0:T(8,128)} %get-tuple-element.12), channel_id=1, source_target_pairs={{0,128},{128,256},{256,384},{384,0},{1,129},{129,257},{257,385},{3... | collective-permute-start | bytes 1376264 | tf_op jit(solution)/shard_map/ppermute | solution.py:156
  50.6 4.5 %collective-permute-start.4 = (f32[128,896]{1,0:T(8,128)}, f32[128,896]{1,0:T(8,128)}, u32[]{:S(2)}, u32[]{:S(2)}) collective-permute-start(f32[128,896]{1,0:T(8,128)} %get-tuple-element.11), channel_id=1, source_target_pairs={{0,384},{128,0},{256,128},{384,256},{1,385},{129,1},{257,129},{385... | collective-permute-start | bytes 1376264 | tf_op jit(solution)/shard_map/ppermute | solution.py:156
  55.1 2.8 %all-to-all-done.1 = f32[64,1,512]{2,1,0:T(1,128)S(1)} async-done(((f32[64,1,512]{2,1,0:T(1,128)}), f32[64,1,512]{2,1,0:T(1,128)S(1)}, u32[]{:S(2)}, u32[]{:S(2)}) %all-to-all-start.1) | async-done | bytes 131104 | tf_op jit(solution)/shard_map/all_to_all | solution.py:143
  57.9 0.1 reduce_sum.18
  58.0 0.7 broadcast_in_dim.12
  58.7 9.8 %all-to-all-start.2 = ((f32[64,1,512]{2,1,0:T(1,128)}), f32[64,1,512]{2,1,0:T(1,128)S(1)}, u32[]{:S(2)}, u32[]{:S(2)}) async-start(f32[64,1,512]{2,1,0:T(1,128)} %broadcast_in_dim.12), calls=%async_computation.2 | async-start | bytes 262144 | tf_op jit(solution)/shard_map/all_to_all | solution.py:143
  68.5 0.0 collective-permute-done.2
  68.5 1.3 collective-permute-done.3
  69.9 0.0 collective-permute-done.4
  69.9 2.0 %fusion.1 = f32[16,8,896]{2,1,0:T(8,128)} fusion(f32[128,896]{1,0:T(8,128)S(1)} %collective-permute-done.2, f32[128,896]{1,0:T(8,128)} %collective-permute-done.3, f32[128,896]{1,0:T(8,128)} %collective-permute-done.4, f32[4,128,896]{2,1,0:T(8,128)S(1)} %bitcast.48, s32[]{:T(128)S(6)} %select_n.56), kind=kLoop, calls=%fused_computation.10 | loop fusion | flops 344064 | bytes 2293764 | tf_op jit(solution)/shard_map/reshape | solution.py:163
  71.9 12.0 %all-to-all-done.2 = f32[64,1,512]{2,1,0:T(1,128)S(1)} async-done(((f32[64,1,512]{2,1,0:T(1,128)}), f32[64,1,512]{2,1,0:T(1,128)S(1)}, u32[]{:S(2)}, u32[]{:S(2)}) %all-to-all-start.2) | async-done | bytes 131104 | tf_op jit(solution)/shard_map/all_to_all | solution.py:143
  83.9 3.7 %all-to-all-start.3 = ((f32[16,8,896]{2,1,0:T(8,128)}), f32[16,8,896]{2,1,0:T(8,128)S(1)}, u32[]{:S(2)}, u32[]{:S(2)}) async-start(f32[16,8,896]{2,1,0:T(8,128)} %fusion.1), calls=%async_computation.3 | async-start | bytes 917504 | tf_op jit(solution)/shard_map/all_to_all | solution.py:143
  87.6 13.3 %all-gather = f32[256,1,512]{2,1,0:T(1,128)S(1)} all-gather(f32[64,1,512]{2,1,0:T(1,128)S(1)} %all-to-all-done.2), channel_id=2, replica_groups=mesh['x'=4,'z'=16,'y'=4,'core'=2] {'y'}, dimensions={0}, use_global_device_ids=true | all-gather | bytes 655360 | tf_op jit(solution)/shard_map/all_gather | solution.py:171
  100.9 1.9 %collective-permute-start.1 = (f32[4,64,512]{2,1,0:T(8,128)S(1)}, f32[4,64,512]{2,1,0:T(8,128)S(1)}, u32[]{:S(2)}, u32[]{:S(2)}) collective-permute-start(f32[4,64,512]{2,1,0:T(8,128)S(1)} %bitcast.49), channel_id=1, source_target_pairs={{0,1},{1,0},{2,3},{3,2},{4,5},{5,4},{6,7},{7,6},{8,9},{9,8},{10,11... | collective-permute-start | bytes 1572872 | tf_op jit(solution)/shard_map/ppermute | solution.py:133
  102.8 8.7 %all-to-all-done.3 = f32[16,8,896]{2,1,0:T(8,128)S(1)} async-done(((f32[16,8,896]{2,1,0:T(8,128)}), f32[16,8,896]{2,1,0:T(8,128)S(1)}, u32[]{:S(2)}, u32[]{:S(2)}) %all-to-all-start.3) | async-done | bytes 458784 | tf_op jit(solution)/shard_map/all_to_all | solution.py:143
  111.6 31.3 %all_gather.7 = f32[128,896]{1,0:T(8,128)S(1)} all-gather(f32[8,896]{1,0:T(8,128)S(1)} %reduce_sum.19), channel_id=1, replica_groups=mesh['x'=4,'z'=16,'y'=4,'core'=2] {'z'}, dimensions={0}, use_global_device_ids=true | all-gather | bytes 487424 | tf_op jit(solution)/shard_map/all_gather | solution.py:165
  142.9 1.3 broadcast_in_dim.13
  144.2 4.6 %all-to-all-start.4 = ((f32[4,128,896]{2,1,0:T(8,128)}), f32[4,128,896]{2,1,0:T(8,128)}, u32[]{:S(2)}, u32[]{:S(2)}) async-start(f32[4,128,896]{2,1,0:T(8,128)} %broadcast_in_dim.13), calls=%async_computation.4 | async-start | bytes 3670016 | tf_op jit(solution)/shard_map/all_to_all | solution.py:143
  148.8 0.0 collective-permute-done.1
  148.8 0.1 select_bitcast_fusion.1
  149.0 0.1 pad_maximum_fusion.1
  149.1 0.1 copy.13
  149.1 13.2 %shard_map.49.refs_0_ = f32[512,1024]{1,0:T(8,128)S(1)} custom-call(f32[512,512]{1,0:T(8,128)S(1)} %bitcast.43), custom_call_target="tpu_custom_call" | custom-call | flops 1610612736 | bytes 4194304 | tf_op jit(solution)/shard_map/pallas_call | solution.py:121
  162.3 13.5 %shard_map.50 = (f32[512,512]{1,0:T(8,128)}, f32[512,512]{1,0:T(8,128)S(1)}) custom-call(f32[512,1024]{1,0:T(8,128)S(1)} %shard_map.49.refs_0_), custom_call_target="tpu_custom_call" | custom-call | flops 1610612736 | bytes 4194304 | tf_op jit(solution)/shard_map/pallas_call | solution.py:121
  175.8 1.8 fusion.4
  177.7 0.0 all-to-all-done.4
  177.7 0.0 copy-start.1
  177.7 5.2 %fusion.3 = f32[512,896]{1,0:T(8,128)S(1)} fusion(f32[512,512]{1,0:T(8,128)S(1)} %get-tuple-element.9, f32[512,896]{1,0:T(8,128)} %bitcast.16), kind=kOutput, calls=%fused_computation.16 | convolution fusion | flops 2818572288 | bytes 4718592 | tf_op jit(solution)/shard_map/dot_general | solution.py:14
  182.9 0.6 constant_dynamic-slice_fusion
  183.5 0.0 copy-done.1
  183.5 3.2 %convolution_subtract_fusion = f32[512,896]{1,0:T(8,128)} fusion(f32[512,896]{1,0:T(8,128)S(1)} %copy-done.1, f32[512,512]{1,0:T(8,128)S(1)} %fusion.4, f32[512,896]{1,0:T(8,128)S(1)} %fusion.3), kind=kOutput, calls=%fused_computation | convolution fusion | flops 1409744896 | bytes 6553600 | tf_op jit(solution)/shard_map/dot_general | solution.py:14
  (2 shorter events, 0.1 us)
Async XLA Ops:
  15.6 3.8 %collective-permute-start = (f32[4,64,512]{2,1,0:T(8,128)S(1)}, f32[4,64,512]{2,1,0:T(8,128)S(1)}, u32[]{:S(2)}, u32[]{:S(2)}) collective-permute-start(f32[4,64,512]{2,1,0:T(8,128)S(1)} %all_to_all.25), channel_id=1, source_target_pairs={{0,1},{1,0},{2,3},{3,2},{4,5},{5,4},{6,7},{7,6},{8,9},{9,8},{10,11... | collective-permute-start | bytes 1572872 | tf_op jit(solution)/shard_map/ppermute | solution.py:133
  17.5 2.1 %copy-start.2 = (f32[512,64]{0,1:T(8,128)S(1)}, f32[512,64]{0,1:T(8,128)}, u32[]{:S(2)}) copy-start(f32[512,64]{0,1:T(8,128)} %param.2) | copy-start | bytes 393220
  19.5 1.5 copy-start
  25.3 32.6 %all-to-all-start.1 = ((f32[64,1,512]{2,1,0:T(1,128)}), f32[64,1,512]{2,1,0:T(1,128)S(1)}, u32[]{:S(2)}, u32[]{:S(2)}) async-start(f32[64,1,512]{2,1,0:T(1,128)} %copy.12), calls=%async_computation.1 | async-start | bytes 262144 | tf_op jit(solution)/shard_map/all_to_all | solution.py:143
  43.0 25.5 %collective-permute-start.2 = (f32[128,896]{1,0:T(8,128)}, f32[128,896]{1,0:T(8,128)S(1)}, u32[]{:S(2)}, u32[]{:S(2)}) collective-permute-start(f32[128,896]{1,0:T(8,128)} %get-tuple-element.13), channel_id=1, source_target_pairs={{0,256},{128,384},{256,0},{384,128},{1,257},{129,385},{257,1},{385... | collective-permute-start | bytes 1376264 | tf_op jit(solution)/shard_map/ppermute | solution.py:156
  48.1 21.8 %collective-permute-start.3 = (f32[128,896]{1,0:T(8,128)}, f32[128,896]{1,0:T(8,128)}, u32[]{:S(2)}, u32[]{:S(2)}) collective-permute-start(f32[128,896]{1,0:T(8,128)} %get-tuple-element.12), channel_id=1, source_target_pairs={{0,128},{128,256},{256,384},{384,0},{1,129},{129,257},{257,385},{3... | collective-permute-start | bytes 1376264 | tf_op jit(solution)/shard_map/ppermute | solution.py:156
  50.6 19.2 %collective-permute-start.4 = (f32[128,896]{1,0:T(8,128)}, f32[128,896]{1,0:T(8,128)}, u32[]{:S(2)}, u32[]{:S(2)}) collective-permute-start(f32[128,896]{1,0:T(8,128)} %get-tuple-element.11), channel_id=1, source_target_pairs={{0,384},{128,0},{256,128},{384,256},{1,385},{129,1},{257,129},{385... | collective-permute-start | bytes 1376264 | tf_op jit(solution)/shard_map/ppermute | solution.py:156
  58.7 25.1 %all-to-all-start.2 = ((f32[64,1,512]{2,1,0:T(1,128)}), f32[64,1,512]{2,1,0:T(1,128)S(1)}, u32[]{:S(2)}, u32[]{:S(2)}) async-start(f32[64,1,512]{2,1,0:T(1,128)} %broadcast_in_dim.12), calls=%async_computation.2 | async-start | bytes 262144 | tf_op jit(solution)/shard_map/all_to_all | solution.py:143
  83.9 27.7 %all-to-all-start.3 = ((f32[16,8,896]{2,1,0:T(8,128)}), f32[16,8,896]{2,1,0:T(8,128)S(1)}, u32[]{:S(2)}, u32[]{:S(2)}) async-start(f32[16,8,896]{2,1,0:T(8,128)} %fusion.1), calls=%async_computation.3 | async-start | bytes 917504 | tf_op jit(solution)/shard_map/all_to_all | solution.py:143
  100.9 47.9 %collective-permute-start.1 = (f32[4,64,512]{2,1,0:T(8,128)S(1)}, f32[4,64,512]{2,1,0:T(8,128)S(1)}, u32[]{:S(2)}, u32[]{:S(2)}) collective-permute-start(f32[4,64,512]{2,1,0:T(8,128)S(1)} %bitcast.49), channel_id=1, source_target_pairs={{0,1},{1,0},{2,3},{3,2},{4,5},{5,4},{6,7},{7,6},{8,9},{9,8},{10,11... | collective-permute-start | bytes 1572872 | tf_op jit(solution)/shard_map/ppermute | solution.py:133
  144.2 33.5 %all-to-all-start.4 = ((f32[4,128,896]{2,1,0:T(8,128)}), f32[4,128,896]{2,1,0:T(8,128)}, u32[]{:S(2)}, u32[]{:S(2)}) async-start(f32[4,128,896]{2,1,0:T(8,128)} %broadcast_in_dim.13), calls=%async_computation.4 | async-start | bytes 3670016 | tf_op jit(solution)/shard_map/all_to_all | solution.py:143
  177.7 5.8 %copy-start.1 = (f32[512,896]{1,0:T(8,128)S(1)}, f32[512,896]{1,0:T(8,128)}, u32[]{:S(2)}) copy-start(f32[512,896]{1,0:T(8,128)} %param.3) | copy-start | bytes 5505028

commit v7 on v6

--- a/solution.py
+++ b/solution.py
@@ -149,17 +149,17 @@
     panel_t = join_cores(exchange(jnp.broadcast_to(block_t, (4, 64, 512)), "y"))
     partial = mxu(panel_t, trailing, ((1,), (0,)))
     gram = mxu(block_t, panel_t, ((1,), (1,)))
-    gram, partial = lax.optimization_barrier((gram, partial))
     blocks, here = partial.reshape(4, 128, width), lax.axis_index("x")
-    away = {}
-    for k in (2, 3, 1):
-        away[k] = lax.ppermute(
+    away = [
+        lax.ppermute(
             lax.dynamic_index_in_dim(blocks, (here + k) % 4, 0, False),
             "x",
             [(i, (i + k) % 4) for i in range(4)],
         )
+        for k in (1, 2, 3)
+    ]
     c = lax.dynamic_index_in_dim(blocks, here, 0, False)
-    c = (c + away[2]) + (away[1] + away[3])
+    c = (c + away[1]) + (away[0] + away[2])
     c = exchange(c.reshape(16, 8, width), "z")
     c = jnp.sum(c, axis=0)
     c = lax.all_gather(c, "z", axis=0, tiled=True)

time: 190 us -> 191 us (level)
  waiting for transfers between devices: 26.7 us -> 23.9 us
  starting transfers between devices: 50.5 us -> 53.3 us
    all_to_all x4, waiting for transfers between devices: 23.5 us -> 17.7 us  [exchange(): return lax.all_to_all(blocks, axes, 0, 0, tiled=True)]
    all_to_all x4, starting transfers between devices: 34.5 us -> 38.6 us  [exchange(): return lax.all_to_all(blocks, axes, 0, 0, tiled=True)]
    ppermute x3, waiting for transfers between devices: 1.35 us -> 4.34 us  [on_device(): lax.ppermute(lax.dynamic_index_in_dim(blocks, (here + k) % 4, 0, False),...]
  transfers between devices with their start and end apart: 9 -> 9, of which waited for: 5 -> 4; matrix products, arithmetic and copies ran while one was open for 4% -> 7% of each run, Pallas kernels for 14% -> 14%
where the time goes in v7:
time: 191 us; the launch traced here: 188 us
  blocking collectives  58.6 us (31%)
  starting transfers between devices  53.3 us (28%)
  Pallas kernels  26.7 us (14%)
  waiting for transfers between devices  23.9 us (13%)
  matrix products  16.4 us (9%)
  local copies, waits for them, and re-layouts  5.67 us (3%)
  other arithmetic  2.6 us (1%)
    all_to_all x4, starting transfers between devices, exchange(): return lax.all_to_all(blocks, axes, 0, 0, tiled=True)  38.6 us
    all_gather x1, blocking collectives, on_device(): c = lax.all_gather(c, 'z', axis=0, tiled=True)  31.3 us
    pallas_call x2, Pallas kernels, factor_steps(): pl.pallas_call(functools.partial(steps_kernel, n, first, last), out_shape...  26.7 us
    all_to_all x4, waiting for transfers between devices, exchange(): return lax.all_to_all(blocks, axes, 0, 0, tiled=True)  17.7 us
    dot_general x5, matrix products, mxu(): lax.dot_general(a, b, (dims, ((), ())), precision=precision, preferred_el...  16.4 us
    all_to_all x1, blocking collectives, exchange(): return lax.all_to_all(blocks, axes, 0, 0, tiled=True)  14 us
    all_gather x1, blocking collectives, on_device(): gram = lax.all_gather(gram.reshape(64, 512), 'y', axis=0, tiled=False)  13.3 us
    ppermute x3, starting transfers between devices, on_device(): lax.ppermute(lax.dynamic_index_in_dim(blocks, (here + k) % 4, 0, False),...  10.9 us
  transfers between devices with their start and end apart: 9, of which 4 were waited for; matrix products, arithmetic and copies ran while one was open for 7% of the time, Pallas kernels for 14%

profile of v7, /device:TPU:24, one launch (start us, length us, event | category | flops | bytes accessed | tf_op | source)
XLA Modules:
  0.0 188.1 jit_solution(5902955418627950053)
XLA Ops:
  0.6 1.0 broadcast_in_dim.11
  1.6 14.0 %all_to_all.25 = f32[4,64,512]{2,1,0:T(8,128)S(1)} all-to-all(f32[4,64,512]{2,1,0:T(8,128)S(1)} %broadcast_in_dim.11), channel_id=1, replica_groups=mesh['x'=4,'z'=16,'y'=4,'core'=2] {'y'}, dimensions={0} | all-to-all | bytes 1048576 | tf_op jit(solution)/shard_map/all_to_all | solution.py:143
  15.6 1.9 %collective-permute-start = (f32[4,64,512]{2,1,0:T(8,128)S(1)}, f32[4,64,512]{2,1,0:T(8,128)S(1)}, u32[]{:S(2)}, u32[]{:S(2)}) collective-permute-start(f32[4,64,512]{2,1,0:T(8,128)S(1)} %all_to_all.25), channel_id=1, source_target_pairs={{0,1},{1,0},{2,3},{3,2},{4,5},{5,4},{6,7},{7,6},{8,9},{9,8},{10,11... | collective-permute-start | bytes 1572872 | tf_op jit(solution)/shard_map/ppermute | solution.py:133
  17.5 0.0 copy-start.1
  17.6 1.8 collective-permute-done
  19.4 0.1 select_bitcast_fusion.3
  19.5 0.1 pad_maximum_fusion
  19.6 0.0 copy-done.1
  19.6 1.1 convolution_bitcast_fusion
  20.8 0.8 copy.13
  21.6 16.5 %all-to-all-start.1 = ((f32[64,1,512]{2,1,0:T(1,128)}), f32[64,1,512]{2,1,0:T(1,128)S(1)}, u32[]{:S(2)}, u32[]{:S(2)}) async-start(f32[64,1,512]{2,1,0:T(1,128)} %copy.13), calls=%async_computation.1 | async-start | bytes 262144 | tf_op jit(solution)/shard_map/all_to_all | solution.py:143
  38.0 5.0 %fusion = f32[4,128,896]{2,1,0:T(8,128)S(1)} fusion(f32[4,128,512]{2,1,0:T(8,128)S(1)} %bitcast.48, f32[512,896]{1,0:T(8,128)} %param.3), kind=kOutput, calls=%fused_computation | convolution fusion | flops 2818572288 | bytes 4718592 | tf_op jit(solution)/shard_map/dot_general | solution.py:14
  43.1 1.1 dynamic-slice_bitcast_fusion
  44.2 4.9 %collective-permute-start.4 = (f32[128,896]{1,0:T(8,128)}, f32[128,896]{1,0:T(8,128)S(1)}, u32[]{:S(2)}, u32[]{:S(2)}) collective-permute-start(f32[128,896]{1,0:T(8,128)} %get-tuple-element.7), channel_id=1, source_target_pairs={{0,384},{128,0},{256,128},{384,256},{1,385},{129,1},{257,129},{385... | collective-permute-start | bytes 1376264 | tf_op jit(solution)/shard_map/ppermute | solution.py:154
  49.1 1.9 %collective-permute-start.3 = (f32[128,896]{1,0:T(8,128)}, f32[128,896]{1,0:T(8,128)}, u32[]{:S(2)}, u32[]{:S(2)}) collective-permute-start(f32[128,896]{1,0:T(8,128)} %get-tuple-element.8), channel_id=1, source_target_pairs={{0,128},{128,256},{256,384},{384,0},{1,129},{129,257},{257,385},{3... | collective-permute-start | bytes 1376264 | tf_op jit(solution)/shard_map/ppermute | solution.py:154
  51.0 4.1 %collective-permute-start.2 = (f32[128,896]{1,0:T(8,128)}, f32[128,896]{1,0:T(8,128)}, u32[]{:S(2)}, u32[]{:S(2)}) collective-permute-start(f32[128,896]{1,0:T(8,128)} %get-tuple-element.9), channel_id=1, source_target_pairs={{0,256},{128,384},{256,0},{384,128},{1,257},{129,385},{257,1},{385... | collective-permute-start | bytes 1376264 | tf_op jit(solution)/shard_map/ppermute | solution.py:154
  55.1 0.0 all-to-all-done.1
  55.2 0.1 reduce_sum.18
  55.3 0.7 broadcast_in_dim.12
  56.0 13.8 %all-to-all-start.2 = ((f32[64,1,512]{2,1,0:T(1,128)}), f32[64,1,512]{2,1,0:T(1,128)S(1)}, u32[]{:S(2)}, u32[]{:S(2)}) async-start(f32[64,1,512]{2,1,0:T(1,128)} %broadcast_in_dim.12), calls=%async_computation.2 | async-start | bytes 262144 | tf_op jit(solution)/shard_map/all_to_all | solution.py:143
  69.8 0.0 collective-permute-done.4
  69.8 4.3 %collective-permute-done.3 = f32[128,896]{1,0:T(8,128)} collective-permute-done((f32[128,896]{1,0:T(8,128)}, f32[128,896]{1,0:T(8,128)}, u32[]{:S(2)}, u32[]{:S(2)}) %collective-permute-start.3) | collective-permute-done | bytes 458784 | tf_op jit(solution)/shard_map/ppermute | solution.py:154
  74.2 0.0 collective-permute-done.2
  74.2 2.0 %fusion.3 = f32[16,8,896]{2,1,0:T(8,128)} fusion(f32[128,896]{1,0:T(8,128)} %collective-permute-done.2, f32[128,896]{1,0:T(8,128)} %collective-permute-done.3, f32[128,896]{1,0:T(8,128)S(1)} %collective-permute-done.4, f32[4,128,896]{2,1,0:T(8,128)S(1)} %fusion, s32[]{:T(128)S(6)} %select_n.56), kind=kLoop, calls=%fused_computation.12 | loop fusion | flops 344064 | bytes 2293764 | tf_op jit(solution)/shard_map/reshape | solution.py:163
  76.2 9.0 %all-to-all-done.2 = f32[64,1,512]{2,1,0:T(1,128)S(1)} async-done(((f32[64,1,512]{2,1,0:T(1,128)}), f32[64,1,512]{2,1,0:T(1,128)S(1)}, u32[]{:S(2)}, u32[]{:S(2)}) %all-to-all-start.2) | async-done | bytes 131104 | tf_op jit(solution)/shard_map/all_to_all | solution.py:143
  85.2 3.7 %all-to-all-start.3 = ((f32[16,8,896]{2,1,0:T(8,128)}), f32[16,8,896]{2,1,0:T(8,128)S(1)}, u32[]{:S(2)}, u32[]{:S(2)}) async-start(f32[16,8,896]{2,1,0:T(8,128)} %fusion.3), calls=%async_computation.3 | async-start | bytes 917504 | tf_op jit(solution)/shard_map/all_to_all | solution.py:143
  88.9 13.3 %all-gather = f32[256,1,512]{2,1,0:T(1,128)S(1)} all-gather(f32[64,1,512]{2,1,0:T(1,128)S(1)} %all-to-all-done.2), channel_id=2, replica_groups=mesh['x'=4,'z'=16,'y'=4,'core'=2] {'y'}, dimensions={0}, use_global_device_ids=true | all-gather | bytes 655360 | tf_op jit(solution)/shard_map/all_gather | solution.py:171
  102.2 1.9 %collective-permute-start.1 = (f32[4,64,512]{2,1,0:T(8,128)S(1)}, f32[4,64,512]{2,1,0:T(8,128)S(1)}, u32[]{:S(2)}, u32[]{:S(2)}) collective-permute-start(f32[4,64,512]{2,1,0:T(8,128)S(1)} %bitcast.50), channel_id=1, source_target_pairs={{0,1},{1,0},{2,3},{3,2},{4,5},{5,4},{6,7},{7,6},{8,9},{9,8},{10,11... | collective-permute-start | bytes 1572872 | tf_op jit(solution)/shard_map/ppermute | solution.py:133
  104.2 8.7 %all-to-all-done.3 = f32[16,8,896]{2,1,0:T(8,128)S(1)} async-done(((f32[16,8,896]{2,1,0:T(8,128)}), f32[16,8,896]{2,1,0:T(8,128)S(1)}, u32[]{:S(2)}, u32[]{:S(2)}) %all-to-all-start.3) | async-done | bytes 458784 | tf_op jit(solution)/shard_map/all_to_all | solution.py:143
  112.9 31.3 %all_gather.7 = f32[128,896]{1,0:T(8,128)S(1)} all-gather(f32[8,896]{1,0:T(8,128)S(1)} %reduce_sum.19), channel_id=1, replica_groups=mesh['x'=4,'z'=16,'y'=4,'core'=2] {'z'}, dimensions={0}, use_global_device_ids=true | all-gather | bytes 487424 | tf_op jit(solution)/shard_map/all_gather | solution.py:165
  144.2 1.3 broadcast_in_dim.13
  145.6 4.6 %all-to-all-start.4 = ((f32[4,128,896]{2,1,0:T(8,128)}), f32[4,128,896]{2,1,0:T(8,128)}, u32[]{:S(2)}, u32[]{:S(2)}) async-start(f32[4,128,896]{2,1,0:T(8,128)} %broadcast_in_dim.13), calls=%async_computation.4 | async-start | bytes 3670016 | tf_op jit(solution)/shard_map/all_to_all | solution.py:143
  150.2 0.0 collective-permute-done.1
  150.2 0.1 select_bitcast_fusion.1
  150.3 0.1 pad_maximum_fusion.1
  150.4 0.1 copy.14
  150.5 13.2 %shard_map.49.refs_0_ = f32[512,1024]{1,0:T(8,128)S(1)} custom-call(f32[512,512]{1,0:T(8,128)S(1)} %bitcast.46), custom_call_target="tpu_custom_call" | custom-call | flops 1610612736 | bytes 4194304 | tf_op jit(solution)/shard_map/pallas_call | solution.py:121
  163.6 13.5 %shard_map.50 = (f32[512,512]{1,0:T(8,128)}, f32[512,512]{1,0:T(8,128)S(1)}) custom-call(f32[512,1024]{1,0:T(8,128)S(1)} %shard_map.49.refs_0_), custom_call_target="tpu_custom_call" | custom-call | flops 1610612736 | bytes 4194304 | tf_op jit(solution)/shard_map/pallas_call | solution.py:121
  177.2 1.8 fusion.5
  179.0 0.0 all-to-all-done.4
  179.0 0.0 copy-start
  179.1 5.2 %fusion.4 = f32[512,896]{1,0:T(8,128)S(1)} fusion(f32[512,512]{1,0:T(8,128)S(1)} %get-tuple-element.6, f32[512,896]{1,0:T(8,128)} %bitcast.17), kind=kOutput, calls=%fused_computation.17 | convolution fusion | flops 2818572288 | bytes 4718592 | tf_op jit(solution)/shard_map/dot_general | solution.py:14
  184.2 0.6 constant_dynamic-slice_fusion
  184.9 0.0 copy-done
  184.9 3.2 %convolution_subtract_fusion = f32[512,896]{1,0:T(8,128)} fusion(f32[512,896]{1,0:T(8,128)S(1)} %copy-done, f32[512,512]{1,0:T(8,128)S(1)} %fusion.5, f32[512,896]{1,0:T(8,128)S(1)} %fusion.4), kind=kOutput, calls=%fused_computation.2 | convolution fusion | flops 1409744896 | bytes 6553600 | tf_op jit(solution)/shard_map/dot_general | solution.py:14
  (2 shorter events, 0.1 us)
Async XLA Ops:
  15.6 3.8 %collective-permute-start = (f32[4,64,512]{2,1,0:T(8,128)S(1)}, f32[4,64,512]{2,1,0:T(8,128)S(1)}, u32[]{:S(2)}, u32[]{:S(2)}) collective-permute-start(f32[4,64,512]{2,1,0:T(8,128)S(1)} %all_to_all.25), channel_id=1, source_target_pairs={{0,1},{1,0},{2,3},{3,2},{4,5},{5,4},{6,7},{7,6},{8,9},{9,8},{10,11... | collective-permute-start | bytes 1572872 | tf_op jit(solution)/shard_map/ppermute | solution.py:133
  17.5 2.1 %copy-start.1 = (f32[512,64]{0,1:T(8,128)S(1)}, f32[512,64]{0,1:T(8,128)}, u32[]{:S(2)}) copy-start(f32[512,64]{0,1:T(8,128)} %param.2) | copy-start | bytes 393220
  21.6 33.6 %all-to-all-start.1 = ((f32[64,1,512]{2,1,0:T(1,128)}), f32[64,1,512]{2,1,0:T(1,128)S(1)}, u32[]{:S(2)}, u32[]{:S(2)}) async-start(f32[64,1,512]{2,1,0:T(1,128)} %copy.13), calls=%async_computation.1 | async-start | bytes 262144 | tf_op jit(solution)/shard_map/all_to_all | solution.py:143
  44.2 25.6 %collective-permute-start.4 = (f32[128,896]{1,0:T(8,128)}, f32[128,896]{1,0:T(8,128)S(1)}, u32[]{:S(2)}, u32[]{:S(2)}) collective-permute-start(f32[128,896]{1,0:T(8,128)} %get-tuple-element.7), channel_id=1, source_target_pairs={{0,384},{128,0},{256,128},{384,256},{1,385},{129,1},{257,129},{385... | collective-permute-start | bytes 1376264 | tf_op jit(solution)/shard_map/ppermute | solution.py:154
  49.1 25.1 %collective-permute-start.3 = (f32[128,896]{1,0:T(8,128)}, f32[128,896]{1,0:T(8,128)}, u32[]{:S(2)}, u32[]{:S(2)}) collective-permute-start(f32[128,896]{1,0:T(8,128)} %get-tuple-element.8), channel_id=1, source_target_pairs={{0,128},{128,256},{256,384},{384,0},{1,129},{129,257},{257,385},{3... | collective-permute-start | bytes 1376264 | tf_op jit(solution)/shard_map/ppermute | solution.py:154
  51.0 23.2 %collective-permute-start.2 = (f32[128,896]{1,0:T(8,128)}, f32[128,896]{1,0:T(8,128)}, u32[]{:S(2)}, u32[]{:S(2)}) collective-permute-start(f32[128,896]{1,0:T(8,128)} %get-tuple-element.9), channel_id=1, source_target_pairs={{0,256},{128,384},{256,0},{384,128},{1,257},{129,385},{257,1},{385... | collective-permute-start | bytes 1376264 | tf_op jit(solution)/shard_map/ppermute | solution.py:154
  56.0 29.2 %all-to-all-start.2 = ((f32[64,1,512]{2,1,0:T(1,128)}), f32[64,1,512]{2,1,0:T(1,128)S(1)}, u32[]{:S(2)}, u32[]{:S(2)}) async-start(f32[64,1,512]{2,1,0:T(1,128)} %broadcast_in_dim.12), calls=%async_computation.2 | async-start | bytes 262144 | tf_op jit(solution)/shard_map/all_to_all | solution.py:143
  85.2 27.7 %all-to-all-start.3 = ((f32[16,8,896]{2,1,0:T(8,128)}), f32[16,8,896]{2,1,0:T(8,128)S(1)}, u32[]{:S(2)}, u32[]{:S(2)}) async-start(f32[16,8,896]{2,1,0:T(8,128)} %fusion.3), calls=%async_computation.3 | async-start | bytes 917504 | tf_op jit(solution)/shard_map/all_to_all | solution.py:143
  102.2 47.9 %collective-permute-start.1 = (f32[4,64,512]{2,1,0:T(8,128)S(1)}, f32[4,64,512]{2,1,0:T(8,128)S(1)}, u32[]{:S(2)}, u32[]{:S(2)}) collective-permute-start(f32[4,64,512]{2,1,0:T(8,128)S(1)} %bitcast.50), channel_id=1, source_target_pairs={{0,1},{1,0},{2,3},{3,2},{4,5},{5,4},{6,7},{7,6},{8,9},{9,8},{10,11... | collective-permute-start | bytes 1572872 | tf_op jit(solution)/shard_map/ppermute | solution.py:133
  145.6 33.5 %all-to-all-start.4 = ((f32[4,128,896]{2,1,0:T(8,128)}), f32[4,128,896]{2,1,0:T(8,128)}, u32[]{:S(2)}, u32[]{:S(2)}) async-start(f32[4,128,896]{2,1,0:T(8,128)} %broadcast_in_dim.13), calls=%async_computation.4 | async-start | bytes 3670016 | tf_op jit(solution)/shard_map/all_to_all | solution.py:143
  179.0 5.8 %copy-start = (f32[512,896]{1,0:T(8,128)S(1)}, f32[512,896]{1,0:T(8,128)}, u32[]{:S(2)}) copy-start(f32[512,896]{1,0:T(8,128)} %param.3) | copy-start | bytes 5505028
